TPU v7x, 256 devices: a whole 4x4x8 slice. The times are simulated.
256 devices in a mesh: dp: 2 (over x_hi), head: 8 (over z), frame: 16 (over y, x_lo, core).
Axes of the slice: x: 4 (x_hi: 2, x_lo: 2; x = x_hi * 2 + x_lo), y: 4, z: 8, core: 2. Of those that a mesh axis runs over, the one named last changes fastest.
Arguments:
- queries: bfloat16 [8192, 5120], P(('dp', 'frame', 'head')), parts along dimension 0, may hold values from -5 to 5
- keys: bfloat16 [8192, 5120], P(('dp', 'frame', 'head')), parts along dimension 0, may hold values from -5 to 5
- values: bfloat16 [8192, 5120], P(('dp', 'frame', 'head')), parts along dimension 0, may hold values from -6 to 6
- out_grad: bfloat16 [8192, 5120], P(('dp', 'frame', 'head')), parts along dimension 0, may hold values from -6 to 6
- tile_mask: int32 [40, 32, 32], P('head'), may hold values from 0 to 1, as said below
Outputs:
- attended: bfloat16 [8192, 5120], P(('dp', 'frame'), 'head'), parts along dimension 0
- query_grad: bfloat16 [8192, 5120], P(('dp', 'frame'), 'head'), parts along dimension 0
- key_grad: bfloat16 [8192, 5120], P(('dp', 'frame'), 'head'), parts along dimension 0
- value_grad: bfloat16 [8192, 5120], P(('dp', 'frame'), 'head'), parts along dimension 0
There are 2 independent parts, one for each index of `dp`. A program takes and returns all parts, laid end to end along the dimension named above; an argument that names none is the same for every part. Nothing has to cross between parts.
Inputs may be any that keep to these rules, and one draw needn't show every extreme that they name: tile_mask[h, i, i] = 1 for every head h and tile i.
All inputs are finite; a program needn't handle non-finite values.
Results may differ from a plain program's by a relative error of at most 0.022.
Values may be sent and summed in bfloat16 or wider, within the bound.
A program may use at most 128 MiB of HBM per device.

v0:
```python
import math

import jax
import jax.numpy as jnp
from jax import lax
from jax.sharding import PartitionSpec as P

HD = 128
TILE = 128


EXCLUDED = -1e30


def expand_tiles(live_block, tile_size):
    head_count, query_tiles, key_tiles = live_block.shape
    spread = jnp.broadcast_to(
        live_block[:, :, None, :, None] == 1,
        (head_count, query_tiles, tile_size, key_tiles, tile_size),
    )
    return spread.reshape(head_count, query_tiles * tile_size, key_tiles * tile_size)


def local(queries, keys, values, out_grad, tile_mask):
    frame_index = lax.axis_index("frame")
    frame_count = lax.axis_size("frame")
    query_rows, key_rows, value_rows, grad_rows = (
        lax.all_to_all(queries, "head", split_axis=1, concat_axis=0, tiled=True),
        lax.all_to_all(keys, "head", split_axis=1, concat_axis=0, tiled=True),
        lax.all_to_all(values, "head", split_axis=1, concat_axis=0, tiled=True),
        lax.all_to_all(out_grad, "head", split_axis=1, concat_axis=0, tiled=True),
    )
    slab_rows = query_rows.shape[0]
    groups = query_rows.shape[1] // HD
    token_count = slab_rows * frame_count
    scaling = 1.0 / math.sqrt(HD)
    query_heads = query_rows.reshape(slab_rows, groups, HD)
    grad_heads = grad_rows.reshape(slab_rows, groups, HD)
    query_tiles = slab_rows // TILE
    mask_rows = lax.dynamic_slice_in_dim(tile_mask, frame_index * query_tiles, query_tiles, 1)

    def blocked(step, initial, piece):
        piece_rows = piece[0].shape[0]
        block_width = slab_rows * math.gcd(piece_rows // slab_rows, 4)

        def one_block(block_index, running_state):
            offset = block_index * block_width
            key_block = lax.dynamic_slice_in_dim(piece[0], offset, block_width, 0).reshape(
                block_width, groups, HD
            )
            value_block = lax.dynamic_slice_in_dim(piece[1], offset, block_width, 0).reshape(
                block_width, groups, HD
            )
            live_block = lax.dynamic_slice_in_dim(mask_rows, offset // TILE, block_width // TILE, 2)
            return step(running_state, key_block, value_block, live_block, offset, 0, groups)

        return lax.fori_loop(0, piece_rows // block_width, one_block, initial)

    def forward_step(
        running_state, key_block, value_block, live_block, block_start, head_lo, head_hi
    ):
        running, totals, summed = running_state
        allowed = expand_tiles(live_block, TILE)
        scores = (
            jnp.einsum("qhd,khd->hqk", query_heads, key_block, preferred_element_type=jnp.float32)
            * scaling
        )
        masked = jnp.where(allowed, scores, EXCLUDED)
        new_running = jnp.maximum(running, jnp.max(masked, axis=2))
        weights = jnp.where(allowed, jnp.exp(masked - new_running[:, :, None]), 0.0)
        factor = jnp.exp(running - new_running)
        new_totals = totals * factor + jnp.sum(weights, axis=2)
        update = jnp.einsum(
            "hqk,khd->qhd",
            weights.astype(jnp.bfloat16),
            value_block,
            preferred_element_type=jnp.float32,
        )
        new_summed = summed * factor.T[:, :, None] + update
        return (
            running.at[head_lo:head_hi].set(new_running),
            totals.at[head_lo:head_hi].set(new_totals),
            summed.at[:, head_lo:head_hi].set(new_summed),
        )

    initial_forward = (
        jnp.full((groups, slab_rows), EXCLUDED, jnp.float32),
        jnp.zeros((groups, slab_rows), jnp.float32),
        jnp.zeros((slab_rows, groups, HD), jnp.float32),
    )
    running, totals, summed = blocked(
        forward_step,
        initial_forward,
        (
            lax.all_gather(key_rows, "frame", axis=0, tiled=True),
            lax.all_gather(value_rows, "frame", axis=0, tiled=True),
        ),
    )
    attended = (summed / totals.T[:, :, None]).astype(jnp.bfloat16)
    logsum = running + jnp.log(totals)
    out_delta = jnp.sum(grad_heads.astype(jnp.float32) * attended.astype(jnp.float32), axis=2).T

    def backward_step(
        running_state, key_block, value_block, live_block, block_start, head_lo, head_hi
    ):
        query_acc, key_acc, value_acc = running_state
        block_width = key_block.shape[0]
        head_count = head_hi - head_lo
        allowed = expand_tiles(live_block, TILE)
        scores = (
            jnp.einsum("qhd,khd->hqk", query_heads, key_block, preferred_element_type=jnp.float32)
            * scaling
        )
        masked = jnp.where(allowed, scores, EXCLUDED)
        probabilities = jnp.where(allowed, jnp.exp(masked - logsum[head_lo:head_hi, :, None]), 0.0)
        prob_grad = jnp.einsum(
            "qhd,khd->hqk", grad_heads, value_block, preferred_element_type=jnp.float32
        )
        score_grad = probabilities * (prob_grad - out_delta[head_lo:head_hi, :, None])
        probs_half = probabilities.astype(jnp.bfloat16)
        score_half = score_grad.astype(jnp.bfloat16)
        value_part = jnp.einsum(
            "hqk,qhd->khd", probs_half, grad_heads, preferred_element_type=jnp.float32
        )
        key_part = (
            jnp.einsum("hqk,qhd->khd", score_half, query_heads, preferred_element_type=jnp.float32)
            * scaling
        )
        query_new = query_acc + jnp.einsum(
            "hqk,khd->qhd", score_half, key_block, preferred_element_type=jnp.float32
        )
        query_acc = query_acc.at[:, head_lo:head_hi].set(query_new)
        key_acc = lax.dynamic_update_slice(
            key_acc, key_part.reshape(block_width, head_count * HD), (block_start, head_lo * HD)
        )
        value_acc = lax.dynamic_update_slice(
            value_acc, value_part.reshape(block_width, head_count * HD), (block_start, head_lo * HD)
        )
        return (query_acc, key_acc, value_acc)

    initial_backward = (
        jnp.zeros((slab_rows, groups, HD), jnp.float32),
        jnp.zeros((token_count, groups * HD), jnp.float32),
        jnp.zeros((token_count, groups * HD), jnp.float32),
    )
    query_acc, key_acc, value_acc = blocked(
        backward_step,
        initial_backward,
        (
            lax.all_gather(key_rows, "frame", axis=0, tiled=True),
            lax.all_gather(value_rows, "frame", axis=0, tiled=True),
        ),
    )
    key_sum, value_sum = (
        lax.psum_scatter(
            key_acc.astype(jnp.bfloat16), "frame", scatter_dimension=0, tiled=True
        ).astype(jnp.float32),
        lax.psum_scatter(
            value_acc.astype(jnp.bfloat16), "frame", scatter_dimension=0, tiled=True
        ).astype(jnp.float32),
    )
    attended_out = attended.reshape(slab_rows, groups * HD)
    query_out = (query_acc * scaling).astype(jnp.bfloat16).reshape(slab_rows, groups * HD)
    return (attended_out, query_out, key_sum.astype(jnp.bfloat16), value_sum.astype(jnp.bfloat16))


def solution(mesh):
    return jax.shard_map(
        local,
        mesh=mesh,
        in_specs=(
            P(("dp", "frame", "head"), None),
            P(("dp", "frame", "head"), None),
            P(("dp", "frame", "head"), None),
            P(("dp", "frame", "head"), None),
            P("head", None, None),
        ),
        out_specs=(
            P(("dp", "frame"), "head"),
            P(("dp", "frame"), "head"),
            P(("dp", "frame"), "head"),
            P(("dp", "frame"), "head"),
        ),
        check_vma=False,
    )
```

profile of v0, /device:TPU:1, one launch (start us, length us, event | category | flops | bytes accessed | tf_op | source)
XLA Modules:
  0.0 400.1 jit_solution(4356435640391929828)
XLA Ops:
  8.2 20.7 %all_to_all.70 = bf16[32,8,640]{2,0,1:T(8,128)(2,1)} all-to-all(bf16[32,8,640]{2,0,1:T(8,128)(2,1)S(1)} %bitcast.165), channel_id=1, replica_groups=mesh['dp'=2,'head'=8,'frame'=16] {'head'}, dimensions={1} | all-to-all | bytes 655360 | tf_op jit(solution)/shard_map/all_to_all | solution.py:29
  30.0 13.1 %all_to_all.71 = bf16[32,8,640]{2,0,1:T(8,128)(2,1)} all-to-all(bf16[32,8,640]{2,0,1:T(8,128)(2,1)S(1)} %bitcast.166), channel_id=1, replica_groups=mesh['dp'=2,'head'=8,'frame'=16] {'head'}, dimensions={1} | all-to-all | bytes 655360 | tf_op jit(solution)/shard_map/all_to_all | solution.py:30
  43.1 1.7 copy.161
  44.8 3.4 all-to-all-start.1
  48.2 1.7 copy.159
  50.0 8.3 %all-to-all-done.1 = bf16[32,8,640]{2,0,1:T(8,128)(2,1)S(1)} async-done(((bf16[32,8,640]{2,0,1:T(8,128)(2,1)}), bf16[32,8,640]{2,0,1:T(8,128)(2,1)S(1)}, u32[]{:S(2)}, u32[]{:S(2)}) %all-to-all-start.1) | async-done | bytes 327712 | tf_op jit(solution)/shard_map/all_to_all | solution.py:28
  58.3 3.4 all-to-all-start.3
  62.6 9.2 %all-to-all-done.3 = bf16[32,8,640]{2,0,1:T(8,128)(2,1)S(1)} async-done(((bf16[32,8,640]{2,0,1:T(8,128)(2,1)}), bf16[32,8,640]{2,0,1:T(8,128)(2,1)S(1)}, u32[]{:S(2)}, u32[]{:S(2)}) %all-to-all-start.3) | async-done | bytes 327712 | tf_op jit(solution)/shard_map/all_to_all | solution.py:31
  73.2 8.0 %copy.124 = bf16[4096,640]{0,1:T(8,128)(2,1)} copy(bf16[4096,640]{1,0:T(8,128)(2,1)} %all-gather.3.cloned.1.call-done) | data formatting | bytes 10485760
  81.2 32.0 %all-gather.5.cloned.1.call-done = bf16[4096,640]{1,0:T(8,128)(2,1)} async-done(((bf16[256,640]{1,0:T(8,128)(2,1)}), bf16[4096,640]{1,0:T(8,128)(2,1)}) %all-gather.5.cloned.1.call-update) | async-done | bytes 5242896 | tf_op jit(solution)/shard_map/all_gather | solution.py:96
  113.2 8.0 %copy.126 = bf16[4096,640]{0,1:T(8,128)(2,1)} copy(bf16[4096,640]{1,0:T(8,128)(2,1)} %all-gather.5.cloned.1.call-done) | data formatting | bytes 10485760
  121.1 41.3 %while.76 = (s32[]{:T(128)}, f32[5,256]{1,0:T(8,128)S(1)}, f32[5,256]{1,0:T(8,128)S(1)}, f32[256,5,128]{0,2,1:T(8,128)}, s32[5,2,32]{2,1,0:T(2,128)S(1)}, /*inde...) while((s32[]{:T(128)}, f32[5,256]{1,0:T(8,128)S(1)}, ...), condition=%wide.region_3.4_spmd.clone, body=%wide.region_0.3_spmd.clone.sunk | while | flops 688629888 | bytes 41053088 | solution.py:57
  121.6 1.5 reshape.285
  123.1 1.4 copy.167
  124.5 2.0 constant_dynamic-slice_fusion.8
  127.8 2.0 fusion.75
  129.8 1.5 fusion.72
  131.9 1.5 reshape.285
  133.4 1.4 copy.167
  134.8 2.0 constant_dynamic-slice_fusion.8
  138.1 2.0 fusion.75
  140.2 1.5 fusion.72
  142.3 1.5 reshape.285
  143.7 1.4 copy.167
  145.2 2.0 constant_dynamic-slice_fusion.8
  148.5 2.0 fusion.75
  150.5 1.5 fusion.72
  152.6 1.5 reshape.285
  154.1 1.4 copy.167
  155.5 2.0 constant_dynamic-slice_fusion.8
  158.8 2.0 fusion.75
  160.8 1.5 fusion.72
  162.4 2.0 multiply_reduce_fusion
  164.4 2.7 broadcast.175.clone2
  167.1 2.8 broadcast.175.clone
  169.9 71.6 %while.77 = (s32[]{:T(128)}, f32[256,5,128]{0,2,1:T(8,128)}, bf16[4096,640]{1,0:T(8,128)(2,1)}, bf16[4096,640]{1,0:T(8,128)(2,1)}, bf16[4096,640]{0,1:T(8,128)(2...) while((s32[]{:T(128)}, f32[256,5,128]{0,2,1:T(8,128)}, ...), condition=%wide.region_6.7_spmd.clone, body=%wide.region_5.6_spmd.clone.sunk | while | flops 1695088768 | bytes 62930880 | solution.py:57
  170.4 1.5 reshape.286
  171.8 1.4 copy.168
  173.3 1.4 constant_dynamic-slice_fusion.10
  174.7 1.4 constant_dynamic-slice_fusion.9
  177.0 2.2 fusion.87
  179.2 2.7 fusion.89
  184.3 1.7 copy.169
  186.0 1.7 constant_dynamic-update-slice_fusion.3
  188.2 1.5 reshape.286
  189.7 1.4 copy.168
  194.9 2.2 fusion.87
  197.1 2.7 fusion.89
  202.2 1.7 copy.169
  203.9 1.8 constant_dynamic-update-slice_fusion.3
  206.2 1.5 reshape.286
  207.7 1.4 copy.168
  212.8 2.2 fusion.87
  215.0 2.7 fusion.89
  220.2 1.7 copy.169
  221.9 1.8 constant_dynamic-update-slice_fusion.3
  224.1 1.5 reshape.286
  225.6 1.4 copy.168
  230.8 2.2 fusion.87
  232.9 2.7 fusion.89
  238.1 1.7 copy.169
  239.8 1.7 constant_dynamic-update-slice_fusion.3
  244.3 71.3 %reduce-scatter.5.cloned.1.call-done = bf16[256,640]{1,0:T(8,128)(2,1)} async-done(((bf16[4096,640]{1,0:T(8,128)(2,1)}), bf16[256,640]{1,0:T(8,128)(2,1)}) %reduce-scatter.5.cloned.1.call-update) | async-done | bytes 327696 | tf_op jit(solution)/shard_map/reduce_scatter | solution.py:158
  315.6 77.9 %reduce-scatter.3.cloned.1.call-done = bf16[256,640]{1,0:T(8,128)(2,1)} async-done(((bf16[4096,640]{1,0:T(8,128)(2,1)}), bf16[256,640]{1,0:T(8,128)(2,1)}) %reduce-scatter.3.cloned.1.call-update) | async-done | bytes 327696 | tf_op jit(solution)/shard_map/reduce_scatter | solution.py:155
  (125 shorter events, 37.8 us)
Async XLA Ops:
  7.2 54.7 %copy-start = (s32[5,32,32]{2,1,0:T(8,128)S(1)}, s32[5,32,32]{2,1,0:T(8,128)}, u32[]{:S(2)}) copy-start(s32[5,32,32]{2,1,0:T(8,128)} %param.29) | copy-start | bytes 61444
  7.2 66.0 %all-gather.3.cloned.1.call-start = ((), (), s32[]{:S(2)}) async-start(), calls=%async_computation.6 | async-start | bytes 5570560 | tf_op jit(solution)/shard_map/all_gather | solution.py:95
  28.9 84.3 %all-gather.5.cloned.1.call-start = ((), (), s32[]{:S(2)}) async-start(), calls=%async_computation.7 | async-start | bytes 5570560 | tf_op jit(solution)/shard_map/all_gather | solution.py:96
  44.8 13.5 %all-to-all-start.1 = ((bf16[32,8,640]{2,0,1:T(8,128)(2,1)}), bf16[32,8,640]{2,0,1:T(8,128)(2,1)S(1)}, u32[]{:S(2)}, u32[]{:S(2)}) async-start(bf16[32,8,640]{2,0,1:T(8,128)(2,1)} %bitcast.96), calls=%async_computation.1 | async-start | bytes 655360 | tf_op jit(solution)/shard_map/all_to_all | solution.py:28
  58.3 13.5 %all-to-all-start.3 = ((bf16[32,8,640]{2,0,1:T(8,128)(2,1)}), bf16[32,8,640]{2,0,1:T(8,128)(2,1)S(1)}, u32[]{:S(2)}, u32[]{:S(2)}) async-start(bf16[32,8,640]{2,0,1:T(8,128)(2,1)} %bitcast.94), calls=%async_computation.3 | async-start | bytes 655360 | tf_op jit(solution)/shard_map/all_to_all | solution.py:31
  61.8 253.9 %reduce-scatter.5.cloned.1.call-start = ((), (), s32[]{:S(2)}) async-start(), calls=%async_computation.9 | async-start | bytes 5570560 | tf_op jit(solution)/shard_map/reduce_scatter | solution.py:158
  126.5 1.3 copy-start.7
  129.8 1.6 copy-start.8
  136.8 1.3 copy-start.7
  140.1 1.6 copy-start.8
  147.1 1.3 copy-start.7
  150.5 1.6 copy-start.8
  157.5 1.3 copy-start.7
  160.8 1.6 copy-start.8
  164.4 5.5 %copy-start.5 = (bf16[256,5,128]{0,2,1:T(8,128)(2,1)S(1)}, bf16[256,5,128]{0,2,1:T(8,128)(2,1)}, u32[]{:S(2)}) copy-start(bf16[256,5,128]{0,2,1:T(8,128)(2,1)} %copy.132) | copy-start | bytes 983044
  179.2 2.7 copy-start.2
  182.6 1.0 copy-start.3
  197.1 2.7 copy-start.2
  200.4 1.0 copy-start.3
  215.0 2.7 copy-start.2
  218.4 1.0 copy-start.3
  232.9 2.7 copy-start.2
  236.3 1.0 copy-start.3
  241.5 152.1 %copy-start.1 = (s32[5,32,32]{2,1,0:T(8,128)S(1)}, s32[5,32,32]{2,1,0:T(8,128)}, u32[]{:S(2)}) copy-start(s32[5,32,32]{2,1,0:T(8,128)} %param.29) | copy-start | bytes 61444
  241.5 1.0 copy-start.6
  241.5 1.9 copy-start.4
  241.5 152.1 %reduce-scatter.3.cloned.1.call-start = ((), (), s32[]{:S(2)}) async-start(), calls=%async_computation.8 | async-start | bytes 5570560 | tf_op jit(solution)/shard_map/reduce_scatter | solution.py:155
Sparse Core Ops, SparseCore 0:
  29.0 40.1 all-gather.2
  71.1 42.0 all-gather.4
  241.6 73.9 reduce-scatter.4
  318.6 74.8 reduce-scatter.2
where the time goes:
time: 402 us; the launch traced here: 400 us
  waiting for transfers between devices  199 us (50%)
  local copies, waits for them, and re-layouts  93.5 us (23%)
  matrix products  42.7 us (11%)
  blocking collectives  33.7 us (8%)
  between operations  13.9 us (3%)
  other arithmetic  8.96 us (2%)
  starting transfers between devices  7.03 us (2%)
    reduce_scatter x1, waiting for transfers between devices, local(): lax.psum_scatter(key_acc.astype(jnp.bfloat16), 'frame', scatter_dimension...  77.9 us
    reduce_scatter x1, waiting for transfers between devices, local(): lax.psum_scatter(value_acc.astype(jnp.bfloat16), 'frame', scatter_dimensi...  71.3 us
    all_gather x1, waiting for transfers between devices, local(): lax.all_gather(value_rows, 'frame', axis=0, tiled=True)  32 us
    reshape x16, local copies, waits for them, and re-layouts, expand_tiles(): spread.reshape(head_count, query_tiles * tile_size, key_tiles * tile_size)  23 us
    all_to_all x1, blocking collectives, local(): lax.all_to_all(keys, 'head', split_axis=1, concat_axis=0, tiled=True)  20.7 us
    unnamed x17, local copies, waits for them, and re-layouts  19.5 us
    dynamic_update_slice x8, local copies, waits for them, and re-layouts, backward_step(): lax.dynamic_update_slice(value_acc, value_part.reshape(block_width, head_...  13.8 us
    dynamic_slice x8, local copies, waits for them, and re-layouts, one_block(): lax.dynamic_slice_in_dim(piece[1], offset, block_width, 0)  13.5 us
  transfers between devices with their start and end apart: 6, of which 5 were waited for; matrix products, arithmetic and copies ran while one was open for 4% of the time, Pallas kernels for 0%

commit v1 on v0

v1 whole, which is shorter than its diff:
```python
import functools
import math

import jax
import jax.numpy as jnp
from jax import lax
from jax.experimental import pallas as pl
from jax.experimental.pallas import tpu as pltpu
from jax.sharding import PartitionSpec as P

HD = 128
TILE = 128
NEG = -1e30
FLOOR = -1e20
LOG2E = 1.4426950408889634
MESH = pl.DeviceIdType.MESH
F32 = jnp.float32
BF16 = jnp.bfloat16

NT = (((1,), (1,)), ((), ()))
NN = (((1,), (0,)), ((), ()))
TN = (((0,), (0,)), ((), ()))

Q, K, V, G = 0, 1, 2, 3


def dot(a, b, dims):
    return lax.dot_general(a, b, dims, preferred_element_type=F32)


def kernel(
    groups,
    q_hbm, k_hbm, v_hbm, g_hbm, mask_ref,
    att_out, dq_out, dk_out, dv_out,
    allx, probs, grads, bias, rows, stats, facts, afacts,
    att_send, dq_send, dk_send, dv_send, out_recv, scaled,
    a2a_send, a2a_recv, own_sem, fwd_send, fwd_recv, st_send, st_recv, out_send, out_rsem,
):
    z = lax.axis_index("head")
    nz = lax.axis_size("head")
    f = lax.axis_index("frame")
    y, xc = f // 4, f % 4
    chunk = q_hbm.shape[0]
    slab = chunk * nz
    width = groups * HD
    scaling = 1.0 / math.sqrt(HD)
    c2 = scaling * LOG2E
    inputs = (q_hbm, k_hbm, v_hbm, g_hbm)

    def head_peer(d):
        return lax.rem(z + d, nz)

    def y_peer(i):
        return lax.rem(y + i, 4) * 4 + xc

    def q_peer(i):
        return y * 4 + lax.rem(xc + i, 4)

    barrier = pltpu.get_barrier_semaphore()
    for d in range(1, nz):
        pl.semaphore_signal(barrier, inc=1, device_id={"head": head_peer(d)}, device_id_type=MESH)
    for i in range(1, 4):
        pl.semaphore_signal(barrier, inc=1, device_id={"frame": y_peer(i)}, device_id_type=MESH)
        pl.semaphore_signal(barrier, inc=1, device_id={"frame": q_peer(i)}, device_id_type=MESH)
    pl.semaphore_wait(barrier, nz - 1 + 6)

    def own_slot(a):
        return y if a in (Q, G) else xc

    def peer(a, i):
        return y_peer(i) if a in (Q, G) else q_peer(i)

    def source_slot(a, i):
        return lax.rem((y if a in (Q, G) else xc) + 4 - i, 4)

    def a2a(a, d):
        to = head_peer(d)
        return pltpu.make_async_remote_copy(
            src_ref=inputs[a].at[:, pl.ds(pl.multiple_of(to * width, width), width)],
            dst_ref=allx.at[a, own_slot(a), pl.ds(pl.multiple_of(z * chunk, chunk), chunk), :],
            send_sem=a2a_send.at[a, d],
            recv_sem=a2a_recv.at[a, d],
            device_id={"head": to},
            device_id_type=MESH,
        )

    def own(a):
        return pltpu.make_async_copy(
            inputs[a].at[:, pl.ds(pl.multiple_of(z * width, width), width)],
            allx.at[a, own_slot(a), pl.ds(pl.multiple_of(z * chunk, chunk), chunk), :],
            own_sem.at[a],
        )

    order = [0]
    for d in range(1, nz // 2 + 1):
        order += [d] if d == nz - d else [d, nz - d]

    for pair in ((K, Q), (V, G)):
        for a in pair:
            own(a).start()
        for d in order[1:]:
            for a in pair:
                a2a(a, d).start()

    def forward(a, d):
        source = lax.rem(z + nz - d, nz)
        part = pl.ds(pl.multiple_of(source * chunk, chunk), chunk)
        for i in (1, 2, 3):
            here = allx.at[a, own_slot(a), part, :]
            pltpu.make_async_remote_copy(
                src_ref=here,
                dst_ref=here,
                send_sem=fwd_send.at[a, i - 1],
                recv_sem=fwd_recv.at[a, i - 1],
                device_id={"frame": peer(a, i)},
                device_id_type=MESH,
            ).start()

    def pass_on(a, d):
        if d == 0:
            own(a).wait()
        else:
            a2a(a, d).wait_recv()
        forward(a, d)

    def slab_copy(a, i):
        return pltpu.make_async_remote_copy(
            src_ref=allx.at[a, own_slot(a)],
            dst_ref=allx.at[a, source_slot(a, i)],
            send_sem=fwd_send.at[a, i - 1],
            recv_sem=fwd_recv.at[a, i - 1],
            device_id={"frame": peer(a, i)},
            device_id_type=MESH,
        )

    def bias_row(row, carry):
        h, qt = row // 8, lax.rem(row, 8)
        qi = (qt // 2) * 8 + xc * 2 + lax.rem(qt, 2)
        for kt in range(8):
            live = mask_ref[h, qi, y * 8 + kt]
            value = jnp.where(live == 1, 0.0, NEG).astype(F32)
            bias[row, :, kt * TILE:(kt + 1) * TILE] = jnp.full((8, TILE), value, F32)
        return carry

    lax.fori_loop(0, groups * 8, bias_row, 0)

    for d in order:
        for a in (K, Q):
            pass_on(a, d)
    for a in (K, Q):
        for i in (1, 2, 3):
            slab_copy(a, i).wait_recv()

    lane = lax.broadcasted_iota(jnp.int32, (slab, HD), 1)

    def softmax_step(unit):
        h, s = unit // 4, lax.rem(unit, 4)
        cols = pl.ds(pl.multiple_of(h * HD, HD), HD)
        query = allx[Q, s, :, cols]
        key = allx[K, :, :, cols].reshape(4 * slab, HD)
        raw = dot(query, key, NT) * c2
        top = raw[:TILE] + bias[h * 8 + 2 * s, 0:1, :]
        low = raw[TILE:] + bias[h * 8 + 2 * s + 1, 0:1, :]
        for part, block in ((0, top), (1, low)):
            peak = jnp.maximum(jnp.max(block, axis=1, keepdims=True), FLOOR)
            weight = jnp.exp2(block - peak)
            total = jnp.sum(weight, axis=1, keepdims=True)
            probs[unit, part * TILE:(part + 1) * TILE, :] = weight.astype(BF16)
            here = pl.ds(part * TILE, TILE)
            old = rows[s, here, :]
            ln = lane[:TILE]
            rows[s, here, :] = jnp.where(ln == h, peak, jnp.where(ln == 8 + h, total, old))

    rows[...] = jnp.zeros_like(rows)
    for step in range(nz):
        for a in (V, G):
            pass_on(a, order[step])

        def two(j, carry, step=step):
            softmax_step(step * 2 + j)
            return carry

        lax.fori_loop(0, 2, two, 0)

    def rest(j, carry):
        softmax_step(j)
        return carry

    lax.fori_loop(2 * nz, groups * 4, rest, 0)

    for a in (V, G):
        for i in (1, 2, 3):
            slab_copy(a, i).wait_recv()

    def out_copy(kind, i, h):
        buffer = (att_send, dq_send, dk_send, dv_send)[kind]
        along = y if kind < 2 else xc
        return pltpu.make_async_remote_copy(
            src_ref=buffer.at[lax.rem(along + i, 4), h],
            dst_ref=out_recv.at[kind, i - 1, h],
            send_sem=out_send.at[kind, i - 1],
            recv_sem=out_rsem.at[kind, i - 1],
            device_id={"frame": y_peer(i) if kind < 2 else q_peer(i)},
            device_id_type=MESH,
        )

    def out_all(kind, i):
        buffer = (att_send, dq_send, dk_send, dv_send)[kind]
        return pltpu.make_async_remote_copy(
            src_ref=buffer.at[0],
            dst_ref=out_recv.at[kind, i - 1],
            send_sem=out_send.at[kind, i - 1],
            recv_sem=out_rsem.at[kind, i - 1],
            device_id={"frame": y_peer(i) if kind < 2 else q_peer(i)},
            device_id_type=MESH,
        )

    def attend_step(unit, carry):
        h, s = unit // 4, lax.rem(unit, 4)
        cols = pl.ds(pl.multiple_of(h * HD, HD), HD)
        value = allx[V, :, :, cols].reshape(4 * slab, HD)
        summed = dot(probs[unit], value, NN)
        att_send[s, h] = summed.astype(BF16)
        moved = jnp.sum(allx[G, s, :, cols].astype(F32) * summed, axis=1, keepdims=True)
        rows[s] = jnp.where(lane == 16 + h, moved, rows[s])
        return carry

    lax.fori_loop(0, groups * 4, attend_step, 0)

    for s in range(4):
        stats[y, :, s * slab:(s + 1) * slab] = rows[s].T[:24]

    def stat_copy(i):
        return pltpu.make_async_remote_copy(
            src_ref=stats.at[y],
            dst_ref=stats.at[y],
            send_sem=st_send.at[i - 1],
            recv_sem=st_recv.at[i - 1],
            device_id={"frame": y_peer(i)},
            device_id_type=MESH,
        )

    for i in (1, 2, 3):
        stat_copy(i).start()
    for h in range(groups):
        for i in (1, 2, 3):
            out_copy(0, i, h).start()
    for i in (1, 2, 3):
        pltpu.make_async_remote_copy(
            src_ref=stats.at[y],
            dst_ref=stats.at[lax.rem(y + 4 - i, 4)],
            send_sem=st_send.at[i - 1],
            recv_sem=st_recv.at[i - 1],
            device_id={"frame": y_peer(i)},
            device_id_type=MESH,
        ).wait_recv()

    peaks = [stats[d, 0:8, :] for d in range(4)]
    peak = functools.reduce(jnp.maximum, peaks)
    shares = [jnp.exp2(p - peak) for p in peaks]
    total = sum(stats[d, 8:16, :] * shares[d] for d in range(4))
    inverse = 1.0 / total
    delta = sum(stats[d, 16:24, :] * shares[d] for d in range(4)) * inverse
    mine = jnp.exp2(stats[y, 0:8, :] - peak) * inverse
    packed = jnp.concatenate([mine, mine * delta], axis=0)
    packed = jnp.concatenate([packed, jnp.zeros((HD - 16, 4 * slab), F32)], axis=0)
    for s in range(4):
        facts[s] = packed[:, s * slab:(s + 1) * slab].T
    weighted = jnp.concatenate([share * inverse for share in shares], axis=0)
    for s in range(4):

        @pl.when(y == s)
        def _(s=s):
            block = weighted[:, s * slab:(s + 1) * slab]
            block = jnp.concatenate([block, jnp.zeros((HD - 32, slab), F32)], axis=0)
            afacts[...] = block.T

    def pick(block, index):
        return jnp.sum(jnp.where(lane == index, block, 0.0), axis=1, keepdims=True)

    def backward_head(h, carry):
        cols = pl.ds(pl.multiple_of(h * HD, HD), HD)

        def one(s, inner):
            unit = h * 4 + s
            ratio = pick(facts[s], h)
            shift = pick(facts[s], 8 + h)
            grad = (allx[G, s, :, cols].astype(F32) * ratio).astype(BF16)
            scaled[pl.ds(pl.multiple_of(s * slab, slab), slab), :] = grad
            value = allx[V, :, :, cols].reshape(4 * slab, HD)
            key = allx[K, :, :, cols].reshape(4 * slab, HD)
            moved = dot(grad, value, NT)
            score = (probs[unit].astype(F32) * (moved - shift)).astype(BF16)
            grads[pl.ds(pl.multiple_of(s * slab, slab), slab), :] = score
            dq_send[s, h] = (dot(score, key, NN) * scaling).astype(BF16)
            return inner

        lax.fori_loop(0, 4, one, 0)

        def keyside(t, inner):
            span = pl.ds(pl.multiple_of(t * slab, slab), slab)
            weight = probs[pl.ds(h * 4, 4), :, span].reshape(4 * slab, slab)
            dv_send[t, h] = dot(weight, scaled[...], TN).astype(BF16)
            query = allx[Q, :, :, cols].reshape(4 * slab, HD)
            dk_send[t, h] = (dot(grads[:, span], query, TN) * scaling).astype(BF16)
            return inner

        lax.fori_loop(0, 4, keyside, 0)
        for kind in (1, 2, 3):
            for i in (1, 2, 3):
                out_copy(kind, i, h).start()
        return carry

    lax.fori_loop(0, groups, backward_head, 0)

    for i in (1, 2, 3):
        out_all(0, i).wait_recv()

    factor = afacts[...]
    for h in range(groups):
        value = pick(factor, y * 8 + h) * att_send[y, h].astype(F32)
        for i in (1, 2, 3):
            source = lax.rem(y + 4 - i, 4)
            value += pick(factor, source * 8 + h) * out_recv[0, i - 1, h].astype(F32)
        att_out[:, h * HD:(h + 1) * HD] = value.astype(BF16)

    for kind, buffer, out in ((1, dq_send, dq_out), (2, dk_send, dk_out), (3, dv_send, dv_out)):
        for i in (1, 2, 3):
            out_all(kind, i).wait_recv()
        mine_slot = y if kind == 1 else xc
        for h in range(groups):
            value = buffer[mine_slot, h].astype(F32)
            for i in (1, 2, 3):
                value += out_recv[kind, i - 1, h].astype(F32)
            out[:, h * HD:(h + 1) * HD] = value.astype(BF16)

    for a in (Q, K, V, G):
        for d in order[1:]:
            a2a(a, d).wait_send()
        for i in (1, 2, 3):
            slab_copy(a, i).wait_send()
    for i in (1, 2, 3):
        stat_copy(i).wait_send()
        for kind in range(4):
            out_all(kind, i).wait_send()


def local(queries, keys, values, out_grad, tile_mask):
    groups = tile_mask.shape[0]
    nz = lax.axis_size("head")
    slab = queries.shape[0] * nz
    units = groups * 4
    out = jax.ShapeDtypeStruct((slab, groups * HD), BF16)
    hbm = pl.BlockSpec(memory_space=pl.ANY)
    vmem = pl.BlockSpec(memory_space=pltpu.VMEM)
    dma = pltpu.SemaphoreType.DMA
    send = pltpu.VMEM((4, groups, slab, HD), BF16)
    return pl.pallas_call(
        functools.partial(kernel, groups),
        out_shape=(out,) * 4,
        in_specs=[hbm] * 4 + [pl.BlockSpec(memory_space=pltpu.SMEM)],
        out_specs=(vmem,) * 4,
        scratch_shapes=[
            pltpu.VMEM((4, 4, slab, groups * HD), BF16),
            pltpu.VMEM((units, slab, 4 * slab), BF16),
            pltpu.VMEM((4 * slab, 4 * slab), BF16),
            pltpu.VMEM((groups * 8, 8, 8 * TILE), F32),
            pltpu.VMEM((4, slab, HD), F32),
            pltpu.VMEM((4, 24, 4 * slab), F32),
            pltpu.VMEM((4, slab, HD), F32),
            pltpu.VMEM((slab, HD), F32),
            send, send, send, send,
            pltpu.VMEM((4, 3, groups, slab, HD), BF16),
            pltpu.VMEM((4 * slab, HD), BF16),
            dma((4, nz)), dma((4, nz)), dma((4,)), dma((4, 3)), dma((4, 3)),
            dma((3,)), dma((3,)), dma((4, 3)), dma((4, 3)),
        ],
        compiler_params=pltpu.CompilerParams(
            collective_id=0, has_side_effects=True, vmem_limit_bytes=60 << 20
        ),
    )(queries, keys, values, out_grad, tile_mask)


def solution(mesh):
    return jax.shard_map(
        local,
        mesh=mesh,
        in_specs=(
            P(("dp", "frame", "head"), None),
            P(("dp", "frame", "head"), None),
            P(("dp", "frame", "head"), None),
            P(("dp", "frame", "head"), None),
            P("head", None, None),
        ),
        out_specs=(
            P(("dp", "frame"), "head"),
            P(("dp", "frame"), "head"),
            P(("dp", "frame"), "head"),
            P(("dp", "frame"), "head"),
        ),
        check_vma=False,
    )
```

time: 402 us -> 104 us (0.26)
  waiting for transfers between devices: 199 us -> 0 us
  Pallas kernels: 0 us -> 98.5 us
  local copies, waits for them, and re-layouts: 93.5 us -> 4.68 us
  matrix products: 42.7 us -> 0 us
  blocking collectives: 33.7 us -> 0 us
  between operations: 13.9 us -> 0.65 us
  other arithmetic: 8.96 us -> 0 us
  starting transfers between devices: 7.03 us -> 0 us
    reduce_scatter x2 -> x0, waiting for transfers between devices: 149 us -> none  [the longest x1 77.9 us: local(): lax.psum_scatter(key_acc.astype(jnp.bfloat16), 'frame', scatter_dimension...]
    pallas_call x0 -> x1, Pallas kernels: none -> 98.5 us  [local(): pl.pallas_call(functools.partial(kernel, groups), out_shape=(out,) * 4, i...]
    dot_general x28 -> x0, matrix products: 42.7 us -> none  [the longest x4 10.9 us: backward_step(): jnp.einsum('hqk,qhd->khd', probs_half, grad_heads, preferred_element_type...]
    all_to_all x2 -> x0, blocking collectives: 33.7 us -> none  [the longest x1 20.7 us: local(): lax.all_to_all(keys, 'head', split_axis=1, concat_axis=0, tiled=True)]
    all_gather x2 -> x0, waiting for transfers between devices: 32 us -> none  [the longest x1 32 us: local(): lax.all_gather(value_rows, 'frame', axis=0, tiled=True)]
    reshape x18 -> x0, local copies, waits for them, and re-layouts: 23.8 us -> none  [the longest x16 23 us: expand_tiles(): spread.reshape(head_count, query_tiles * tile_size, key_tiles * tile_size)]
    dynamic_slice x13 -> x0, local copies, waits for them, and re-layouts: 19.2 us -> none  [the longest x8 13.5 us: one_block(): lax.dynamic_slice_in_dim(piece[1], offset, block_width, 0)]
    all_to_all x2 -> x0, waiting for transfers between devices: 17.5 us -> none  [the longest x1 9.2 us: local(): lax.all_to_all(out_grad, 'head', split_axis=1, concat_axis=0, tiled=True)]
  transfers between devices with their start and end apart: 6 -> 0, of which waited for: 5 -> 0; matrix products, arithmetic and copies ran while one was open for 4% -> 0% of each run, Pallas kernels for 0% -> 0%
where the time goes in v1:
time: 104 us
  Pallas kernels  98.5 us (95%)
  local copies, waits for them, and re-layouts  4.68 us (4%)
    pallas_call x1, Pallas kernels, local(): pl.pallas_call(functools.partial(kernel, groups), out_shape=(out,) * 4, i...  98.5 us
    unnamed x10, local copies, waits for them, and re-layouts  4.68 us

profile of v1, /device:TPU:1, one launch (start us, length us, event | category | flops | bytes accessed | tf_op | source)
XLA Modules:
  0.0 103.9 jit_solution(13697999031860569212)
XLA Ops:
  0.6 98.5 %shard_map.84 = (bf16[256,640]{1,0:T(8,128)(2,1)}, bf16[256,640]{1,0:T(8,128)(2,1)}, bf16[256,640]{1,0:T(8,128)(2,1)}, bf16[256,640]{1,0:T(8,128)(2,1)}) custom-call(bf16[32,5120]{1,0:T(8,128)(2,1)} %q_hbm.1, bf16[32,5120]{1,0:T(8,128)(2,1)} %k_hbm.1, bf16[32,5120]{1,0:T(8,128)(2,1)} %v_hbm.1, bf16[32,5120]{1,0:T(8,128)(2,1)} %g_hbm.1, s32[5,32,32]{2,1,0:T(8,128)} %mask_ref.1), custom_call_target="tpu_custom_call" | custom-call | tf_op jit(solution)/shard_map/pallas_call | solution.py:358
  99.2 0.0 copy-start.2
  99.2 1.8 %copy.13 = bf16[256,640]{1,0:T(8,128)(2,1)} copy(bf16[256,640]{1,0:T(8,128)(2,1)} %get-tuple-element.8) | data formatting | bytes 655360
  101.0 0.0 copy-done.2
  101.0 0.0 copy-start.1
  101.0 0.7 copy.14
  101.7 0.4 copy-done.1
  102.1 0.0 copy-start
  102.1 0.7 copy.15
  102.8 0.4 copy-done
  103.2 0.7 copy.16
Async XLA Ops:
  99.2 1.8 %copy-start.2 = (bf16[256,640]{1,0:T(8,128)(2,1)S(1)}, bf16[256,640]{1,0:T(8,128)(2,1)}, u32[]{:S(2)}) copy-start(bf16[256,640]{1,0:T(8,128)(2,1)} %get-tuple-element.9) | copy-start | bytes 983044
  101.0 1.1 %copy-start.1 = (bf16[256,640]{1,0:T(8,128)(2,1)S(1)}, bf16[256,640]{1,0:T(8,128)(2,1)}, u32[]{:S(2)}) copy-start(bf16[256,640]{1,0:T(8,128)(2,1)} %get-tuple-element.10) | copy-start | bytes 983044
  102.1 1.1 %copy-start = (bf16[256,640]{1,0:T(8,128)(2,1)S(1)}, bf16[256,640]{1,0:T(8,128)(2,1)}, u32[]{:S(2)}) copy-start(bf16[256,640]{1,0:T(8,128)(2,1)} %get-tuple-element.11) | copy-start | bytes 983044

commit v2 on v1

v2 whole, which is shorter than its diff:
```python
import functools
import math

import jax
import jax.numpy as jnp
from jax import lax
from jax.experimental import pallas as pl
from jax.experimental.pallas import tpu as pltpu
from jax.sharding import PartitionSpec as P

HD = 128
TILE = 128
NEG = -1e30
FLOOR = -1e20
LOG2E = 1.4426950408889634
MESH = pl.DeviceIdType.MESH
F32 = jnp.float32
BF16 = jnp.bfloat16

NT = (((1,), (1,)), ((), ()))
NN = (((1,), (0,)), ((), ()))
TN = (((0,), (0,)), ((), ()))

Q, K, V, G = 0, 1, 2, 3


def dot(a, b, dims):
    return lax.dot_general(a, b, dims, preferred_element_type=F32)


def kernel(
    groups,
    q_hbm, k_hbm, v_hbm, g_hbm, mask_ref,
    att_out, dq_out, dk_out, dv_out,
    allx, probs, grads, bias, rows, stats, deltas, facts, shifts, scaled, parts, halves, landed,
    a2a_send, a2a_recv, own_sem, near_send, near_recv, relay_send, relay_recv,
    st_send, st_recv, dl_send, dl_recv, half_send, half_recv, land_send, land_recv,
):
    z = lax.axis_index("head")
    nz = lax.axis_size("head")
    f = lax.axis_index("frame")
    y, xc = f // 4, lax.rem(f, 4)
    chunk = q_hbm.shape[0]
    slab = chunk * nz
    width = groups * HD
    scaling = 1.0 / math.sqrt(HD)
    c2 = scaling * LOG2E
    inputs = (q_hbm, k_hbm, v_hbm, g_hbm)

    up, down, far = lax.rem(y + 1, 4), lax.rem(y + 3, 4), lax.rem(y + 2, 4)
    core = lax.rem(xc, 2)
    mate = xc + 1 - 2 * core
    across = lax.rem(xc + 2, 4)
    corner = lax.rem(mate + 2, 4)
    y_near = (up * 4 + xc, down * 4 + xc)
    q_near = (y * 4 + mate, y * 4 + across)

    def near(a):
        return y_near if a in (Q, G) else q_near

    def near_slot(a):
        return (up, down) if a in (Q, G) else (mate, across)

    def own_slot(a):
        return y if a in (Q, G) else xc

    def remote(src, dst, send, recv, frame):
        return pltpu.make_async_remote_copy(
            src_ref=src, dst_ref=dst, send_sem=send, recv_sem=recv,
            device_id={"frame": frame}, device_id_type=MESH,
        )

    barrier = pltpu.get_barrier_semaphore()
    for d in range(1, nz):
        pl.semaphore_signal(
            barrier, inc=1, device_id={"head": lax.rem(z + d, nz)}, device_id_type=MESH
        )
    for frame in (*y_near, far * 4 + xc, *q_near):
        pl.semaphore_signal(barrier, inc=1, device_id={"frame": frame}, device_id_type=MESH)
    pl.semaphore_wait(barrier, nz - 1 + 5)

    def a2a(a, d):
        to = lax.rem(z + d, nz)
        return pltpu.make_async_remote_copy(
            src_ref=inputs[a].at[:, pl.ds(pl.multiple_of(to * width, width), width)],
            dst_ref=allx.at[a, own_slot(a), pl.ds(pl.multiple_of(z * chunk, chunk), chunk), :],
            send_sem=a2a_send.at[a, d],
            recv_sem=a2a_recv.at[a, d],
            device_id={"head": to},
            device_id_type=MESH,
        )

    def own(a):
        return pltpu.make_async_copy(
            inputs[a].at[:, pl.ds(pl.multiple_of(z * width, width), width)],
            allx.at[a, own_slot(a), pl.ds(pl.multiple_of(z * chunk, chunk), chunk), :],
            own_sem.at[a],
        )

    def distance(step):
        if isinstance(step, int):
            return (step + 1) // 2 if step % 2 else (nz - step // 2) % nz
        return jnp.where(lax.rem(step, 2) == 1, (step + 1) // 2, lax.rem(nz - step // 2, nz))

    for pair in ((K, Q), (V, G)):
        for a in pair:
            own(a).start()
        for step in range(1, nz):
            for a in pair:
                a2a(a, distance(step)).start()

    def span(d, lo=0, size=None):
        start = lax.rem(z + nz - d, nz) * chunk + lo
        size = chunk if size is None else size
        return pl.ds(pl.multiple_of(start, size), size)

    def near_copy(a, d, i):
        here = allx.at[a, own_slot(a), span(d), :]
        return remote(here, here, near_send.at[a, i], near_recv.at[a, i, d], near(a)[i])

    def near_arrival(a, d, i):
        there = allx.at[a, near_slot(a)[i], span(d), :]
        back = 1 - i if a in (Q, G) else i
        return remote(there, there, near_send.at[a, i], near_recv.at[a, back, d], near(a)[i])

    def relay_copy(a, d, i):
        half = chunk // 2
        if a in (Q, G):
            part = allx.at[a, near_slot(a)[1 - i], span(d, i * half, half), :]
            return remote(part, part, relay_send.at[a, i], relay_recv.at[a, i], near(a)[i])
        part = allx.at[a, across, span(d), :]
        return remote(part, part, relay_send.at[a, 0], relay_recv.at[a, 0], q_near[0])

    def pass_on(a, d, first=False):
        if first:
            own(a).wait()
        else:
            a2a(a, d).wait_recv()
        for i in (0, 1):
            near_copy(a, d, i).start()

    def relay(a, d):
        if a in (Q, G):
            for i in (0, 1):
                near_arrival(a, d, 1 - i).wait_recv()
                relay_copy(a, d, i).start()
        else:
            near_arrival(a, d, 1).wait_recv()
            relay_copy(a, d, 0).start()

    def relay_total(a, i):
        size = slab // 2 if a in (Q, G) else slab
        part = allx.at[a, 0, 0:size, :]
        return remote(part, part, relay_send.at[a, i], relay_recv.at[a, i], near(a)[i])

    def arrived(a):
        if a in (Q, G):
            for i in (0, 1):
                relay_total(a, i).wait_recv()
        else:
            for step in range(nz):
                near_arrival(a, distance(step), 0).wait_recv()
            relay_total(a, 0).wait_recv()

    def bias_row(row, carry):
        h, qt = row // 8, lax.rem(row, 8)
        qi = (qt // 2) * 8 + xc * 2 + lax.rem(qt, 2)
        for kt in range(8):
            live = mask_ref[h, qi, y * 8 + kt]
            value = jnp.where(live == 1, 0.0, NEG).astype(F32)
            bias[row, :, kt * TILE:(kt + 1) * TILE] = jnp.full((8, TILE), value, F32)
        return carry

    for a in (K, Q):
        pass_on(a, 0, True)
    lax.fori_loop(0, groups * 8, bias_row, 0)
    for step in range(1, nz):
        for a in (K, Q):
            pass_on(a, distance(step))
        for a in (K, Q):
            relay(a, distance(step - 1))
    for a in (K, Q):
        relay(a, distance(nz - 1))
    for a in (V, G):
        pass_on(a, 0, True)
    for a in (K, Q):
        arrived(a)

    lane = lax.broadcasted_iota(jnp.int32, (slab, HD), 1)

    def column(h):
        return pl.ds(pl.multiple_of(h * HD, HD), HD)

    def softmax_step(unit):
        h, s = unit // 4, lax.rem(unit, 4)
        cols = column(h)
        query = allx[Q, s, :, cols]
        key = allx[K, :, :, cols].reshape(4 * slab, HD)
        raw = dot(query, key, NT) * c2
        top = raw[:TILE] + bias[h * 8 + 2 * s, 0:1, :]
        low = raw[TILE:] + bias[h * 8 + 2 * s + 1, 0:1, :]
        for part, block in ((0, top), (1, low)):
            peak = jnp.maximum(jnp.max(block, axis=1, keepdims=True), FLOOR)
            weight = jnp.exp2(block - peak)
            total = jnp.sum(weight, axis=1, keepdims=True)
            probs[unit, part * TILE:(part + 1) * TILE, :] = weight.astype(BF16)
            here = pl.ds(part * TILE, TILE)
            old = rows[s, here, :]
            ln = lane[:TILE]
            rows[s, here, :] = jnp.where(ln == h, peak, jnp.where(ln == 8 + h, total, old))

    rows[...] = jnp.zeros_like(rows)

    def travel_step(step, carry):
        for a in (V, G):
            pass_on(a, distance(step))
        for a in (V, G):
            relay(a, distance(step - 1))

        def one(unit, inner):
            softmax_step(unit)
            return inner

        lax.fori_loop(2 * step - 2, 2 * step, one, 0)
        return carry

    lax.fori_loop(1, nz, travel_step, 0)
    for a in (V, G):
        relay(a, distance(nz - 1))

    def rest(unit, carry):
        softmax_step(unit)
        return carry

    lax.fori_loop(2 * nz - 2, groups * 4, rest, 0)

    for s in range(4):
        stats[y, :, s * slab:(s + 1) * slab] = rows[s].T[:16]

    def stat_copy(i, slot):
        frame = (up * 4 + xc, far * 4 + xc, down * 4 + xc)[i]
        part = stats.at[slot]
        return remote(part, part, st_send.at[i], st_recv.at[i], frame)

    def delta_copy(i, slot):
        frame = (up * 4 + xc, far * 4 + xc, down * 4 + xc)[i]
        part = deltas.at[slot]
        return remote(part, part, dl_send.at[i], dl_recv.at[i], frame)

    for i in range(3):
        stat_copy(i, y).start()
    for a in (V, G):
        arrived(a)
    for i in range(3):
        stat_copy(i, (down, far, up)[i]).wait_recv()

    peaks = [stats[d, 0:8, :] for d in range(4)]
    peak = functools.reduce(jnp.maximum, peaks)
    total = sum(stats[d, 8:16, :] * jnp.exp2(peaks[d] - peak) for d in range(4))
    ratio = jnp.exp2(stats[y, 0:8, :] - peak) / total
    blank = jnp.zeros((HD - 8, slab), F32)
    for s in range(4):
        block = jnp.concatenate([ratio[:, s * slab:(s + 1) * slab], blank], axis=0)
        facts[s] = block.T

    def pick(block, index):
        return jnp.sum(jnp.where(lane == index, block, 0.0), axis=1, keepdims=True)

    ATT, DQ, DK, DV = 0, 1, 2, 3

    def half_copies(kind, h):
        half = slab // 2
        if kind in (ATT, DQ):
            return [
                remote(
                    parts.at[kind, far, h, i * half:(i + 1) * half, :],
                    halves.at[kind, h, i * half:(i + 1) * half, :],
                    half_send.at[kind, i], half_recv.at[kind, h, i], y_near[i],
                )
                for i in (0, 1)
            ]
        return [
            remote(
                parts.at[kind, corner, h], halves.at[kind, h],
                half_send.at[kind, 0], half_recv.at[kind, h, 0], q_near[0],
            )
        ]

    def land_copy(kind, h, i):
        slot = (up, down)[i] if kind in (ATT, DQ) else (mate, across)[i]
        frame = y_near[i] if kind in (ATT, DQ) else q_near[i]
        return remote(
            parts.at[kind, slot, h], landed.at[kind, i, h],
            land_send.at[kind, i], land_recv.at[kind, i], frame,
        )

    def first_stage(kind, h):
        for copy in half_copies(kind, h):
            copy.start()
        if kind in (DK, DV):
            land_copy(kind, h, 0).start()

    def second_stage(kind, h):
        half = slab // 2
        for copy in half_copies(kind, h):
            copy.wait_recv()
        if kind in (ATT, DQ):
            for i in (0, 1):
                slot, part = (up, down)[i], slice(i * half, (i + 1) * half)
                mine = parts[kind, slot, h, part, :].astype(F32)
                parts[kind, slot, h, part, :] = (
                    mine + halves[kind, h, part, :].astype(F32)
                ).astype(BF16)
            for i in (0, 1):
                land_copy(kind, h, i).start()
        else:
            mine = parts[kind, across, h].astype(F32)
            parts[kind, across, h] = (mine + halves[kind, h].astype(F32)).astype(BF16)
            land_copy(kind, h, 1).start()

    def attend_head(h, carry):
        cols = column(h)
        value = allx[V, :, :, cols].reshape(4 * slab, HD)
        for s in range(4):
            factor = pick(facts[s], h)
            summed = dot(probs[h * 4 + s], value, NN) * factor
            parts[ATT, s, h] = summed.astype(BF16)
            grad = allx[G, s, :, cols].astype(F32)
            scaled[h, s * slab:(s + 1) * slab, :] = (grad * factor).astype(BF16)
            moved = jnp.sum(grad * summed, axis=1, keepdims=True)
            rows[s] = jnp.where(lane == 16 + h, moved, rows[s])
        first_stage(ATT, h)
        return carry

    lax.fori_loop(0, groups, attend_head, 0)
    for s in range(4):
        deltas[y, :, s * slab:(s + 1) * slab] = rows[s].T[16:24]
    for i in range(3):
        delta_copy(i, y).start()

    def value_head(h, carry):
        turned = scaled[h].T
        weight = probs[pl.ds(h * 4, 4)].reshape(4 * slab, 4 * slab)
        for t in range(4):
            part = dot(turned, weight[:, t * slab:(t + 1) * slab], NN)
            parts[DV, t, h] = part.T.astype(BF16)
        first_stage(DV, h)
        second_stage(ATT, h)
        return carry

    lax.fori_loop(0, groups, value_head, 0)

    for i in range(3):
        delta_copy(i, (down, far, up)[i]).wait_recv()
    delta = sum(deltas[d] for d in range(4)) * ratio
    for s in range(4):
        block = jnp.concatenate([delta[:, s * slab:(s + 1) * slab], blank], axis=0)
        shifts[s] = block.T

    def backward_head(h, carry):
        cols = column(h)

        def one(s, inner):
            here = pl.ds(pl.multiple_of(s * slab, slab), slab)
            shift = pick(shifts[s], h)
            value = allx[V, :, :, cols].reshape(4 * slab, HD)
            key = allx[K, :, :, cols].reshape(4 * slab, HD)
            moved = dot(scaled[h, here, :], value, NT)
            score = (probs[h * 4 + s].astype(F32) * (moved - shift)).astype(BF16)
            grads[here, :] = score
            parts[DQ, s, h] = (dot(score, key, NN) * scaling).astype(BF16)
            return inner

        lax.fori_loop(0, 4, one, 0)
        first_stage(DQ, h)
        query = allx[Q, :, :, cols].reshape(4 * slab, HD)
        turned = query.T
        for t in range(4):
            part = dot(turned, grads[:, t * slab:(t + 1) * slab], NN)
            parts[DK, t, h] = (part.T * scaling).astype(BF16)
        first_stage(DK, h)
        second_stage(DV, h)

        @pl.when(h > 0)
        def _():
            second_stage(DQ, h - 1)
            second_stage(DK, h - 1)

        return carry

    lax.fori_loop(0, groups, backward_head, 0)
    second_stage(DQ, groups - 1)
    second_stage(DK, groups - 1)

    def land_total(kind, i):
        frame = y_near[i] if kind in (ATT, DQ) else q_near[i]
        return remote(
            parts.at[kind, 0], landed.at[kind, i], land_send.at[kind, i], land_recv.at[kind, i], frame
        )

    def land_arrival(kind, i):
        back = 1 - i if kind in (ATT, DQ) else i
        land_total(kind, back).wait_recv()

    for kind, out in ((ATT, att_out), (DV, dv_out), (DK, dk_out), (DQ, dq_out)):
        for i in (0, 1):
            land_arrival(kind, i)
        slot = y if kind in (ATT, DQ) else xc
        for h in range(groups):
            value = parts[kind, slot, h].astype(F32)
            for i in (0, 1):
                value += landed[kind, i, h].astype(F32)
            out[:, h * HD:(h + 1) * HD] = value.astype(BF16)

    for a in (Q, K, V, G):
        for d in range(1, nz):
            a2a(a, d).wait_send()
        for i in (0, 1):
            part = allx.at[a, 0]
            remote(part, part, near_send.at[a, i], relay_recv.at[a, 0], near(a)[i]).wait_send()
        for i in (0, 1) if a in (Q, G) else (0,):
            relay_total(a, i).wait_send()
    for i in range(3):
        stat_copy(i, y).wait_send()
        delta_copy(i, y).wait_send()
    for kind in range(4):
        for i in (0, 1) if kind in (ATT, DQ) else (0,):
            size = slab // 2 if kind in (ATT, DQ) else slab
            part = parts.at[kind, 0, :, 0:size, :]
            remote(
                part, part, half_send.at[kind, i], half_recv.at[kind, 0, i], y_near[i]
            ).wait_send()
        for i in (0, 1):
            land_total(kind, i).wait_send()


def local(queries, keys, values, out_grad, tile_mask):
    groups = tile_mask.shape[0]
    nz = lax.axis_size("head")
    slab = queries.shape[0] * nz
    units = groups * 4
    out = jax.ShapeDtypeStruct((slab, groups * HD), BF16)
    hbm = pl.BlockSpec(memory_space=pl.ANY)
    vmem = pl.BlockSpec(memory_space=pltpu.VMEM)
    dma = pltpu.SemaphoreType.DMA
    return pl.pallas_call(
        functools.partial(kernel, groups),
        out_shape=(out,) * 4,
        in_specs=[hbm] * 4 + [pl.BlockSpec(memory_space=pltpu.SMEM)],
        out_specs=(vmem,) * 4,
        scratch_shapes=[
            pltpu.VMEM((4, 4, slab, groups * HD), BF16),
            pltpu.VMEM((units, slab, 4 * slab), BF16),
            pltpu.VMEM((4 * slab, 4 * slab), BF16),
            pltpu.VMEM((groups * 8, 8, 8 * TILE), F32),
            pltpu.VMEM((4, slab, HD), F32),
            pltpu.VMEM((4, 16, 4 * slab), F32),
            pltpu.VMEM((4, 8, 4 * slab), F32),
            pltpu.VMEM((4, slab, HD), F32),
            pltpu.VMEM((4, slab, HD), F32),
            pltpu.VMEM((groups, 4 * slab, HD), BF16),
            pltpu.VMEM((4, 4, groups, slab, HD), BF16),
            pltpu.VMEM((4, groups, slab, HD), BF16),
            pltpu.VMEM((4, 2, groups, slab, HD), BF16),
            dma((4, nz)), dma((4, nz)), dma((4,)), dma((4, 2)), dma((4, 2, nz)),
            dma((4, 2)), dma((4, 2)), dma((3,)), dma((3,)), dma((3,)), dma((3,)),
            dma((4, 2)), dma((4, groups, 2)), dma((4, 2)), dma((4, 2)),
        ],
        compiler_params=pltpu.CompilerParams(
            collective_id=0, has_side_effects=True, vmem_limit_bytes=56 << 20
        ),
    )(queries, keys, values, out_grad, tile_mask)


def solution(mesh):
    return jax.shard_map(
        local,
        mesh=mesh,
        in_specs=(
            P(("dp", "frame", "head"), None),
            P(("dp", "frame", "head"), None),
            P(("dp", "frame", "head"), None),
            P(("dp", "frame", "head"), None),
            P("head", None, None),
        ),
        out_specs=(
            P(("dp", "frame"), "head"),
            P(("dp", "frame"), "head"),
            P(("dp", "frame"), "head"),
            P(("dp", "frame"), "head"),
        ),
        check_vma=False,
    )
```

time: 104 us -> 102 us (0.981)
  Pallas kernels: 98.5 us -> 96 us
    pallas_call x1, Pallas kernels: 98.5 us -> 96 us  [local(): pl.pallas_call(functools.partial(kernel, groups), out_shape=(out,) * 4, i...]
where the time goes in v2:
time: 102 us; the launch traced here: 101 us
  Pallas kernels  96 us (94%)
  local copies, waits for them, and re-layouts  4.68 us (5%)
    pallas_call x1, Pallas kernels, local(): pl.pallas_call(functools.partial(kernel, groups), out_shape=(out,) * 4, i...  96 us
    unnamed x10, local copies, waits for them, and re-layouts  4.68 us

profile of v2, /device:TPU:1, one launch (start us, length us, event | category | flops | bytes accessed | tf_op | source)
XLA Modules:
  0.0 101.4 jit_solution(5497242866957620817)
XLA Ops:
  0.6 96.0 %shard_map.84 = (bf16[256,640]{1,0:T(8,128)(2,1)}, bf16[256,640]{1,0:T(8,128)(2,1)}, bf16[256,640]{1,0:T(8,128)(2,1)}, bf16[256,640]{1,0:T(8,128)(2,1)}) custom-call(bf16[32,5120]{1,0:T(8,128)(2,1)} %q_hbm.1, bf16[32,5120]{1,0:T(8,128)(2,1)} %k_hbm.1, bf16[32,5120]{1,0:T(8,128)(2,1)} %v_hbm.1, bf16[32,5120]{1,0:T(8,128)(2,1)} %g_hbm.1, s32[5,32,32]{2,1,0:T(8,128)} %mask_ref.1), custom_call_target="tpu_custom_call" | custom-call | tf_op jit(solution)/shard_map/pallas_call | solution.py:446
  96.7 0.0 copy-start.2
  96.7 1.8 %copy.13 = bf16[256,640]{1,0:T(8,128)(2,1)} copy(bf16[256,640]{1,0:T(8,128)(2,1)} %get-tuple-element.8) | data formatting | bytes 655360
  98.5 0.0 copy-done.2
  98.5 0.0 copy-start.1
  98.5 0.7 copy.14
  99.2 0.4 copy-done.1
  99.5 0.0 copy-start
  99.5 0.7 copy.15
  100.3 0.4 copy-done
  100.6 0.7 copy.16
Async XLA Ops:
  96.7 1.8 %copy-start.2 = (bf16[256,640]{1,0:T(8,128)(2,1)S(1)}, bf16[256,640]{1,0:T(8,128)(2,1)}, u32[]{:S(2)}) copy-start(bf16[256,640]{1,0:T(8,128)(2,1)} %get-tuple-element.9) | copy-start | bytes 983044
  98.5 1.1 %copy-start.1 = (bf16[256,640]{1,0:T(8,128)(2,1)S(1)}, bf16[256,640]{1,0:T(8,128)(2,1)}, u32[]{:S(2)}) copy-start(bf16[256,640]{1,0:T(8,128)(2,1)} %get-tuple-element.10) | copy-start | bytes 983044
  99.5 1.1 %copy-start = (bf16[256,640]{1,0:T(8,128)(2,1)S(1)}, bf16[256,640]{1,0:T(8,128)(2,1)}, u32[]{:S(2)}) copy-start(bf16[256,640]{1,0:T(8,128)(2,1)} %get-tuple-element.11) | copy-start | bytes 983044

commit v3 on v2

--- a/solution.py
+++ b/solution.py
@@ -33,7 +33,7 @@
     q_hbm, k_hbm, v_hbm, g_hbm, mask_ref,
     att_out, dq_out, dk_out, dv_out,
     allx, probs, grads, bias, rows, stats, deltas, facts, shifts, scaled, parts, halves, landed,
-    a2a_send, a2a_recv, own_sem, near_send, near_recv, relay_send, relay_recv,
+    a2a_send, a2a_recv, own_sem, near_send, near_recv,
     st_send, st_recv, dl_send, dl_recv, half_send, half_recv, land_send, land_recv,
 ):
     z = lax.axis_index("head")
@@ -55,12 +55,6 @@
     y_near = (up * 4 + xc, down * 4 + xc)
     q_near = (y * 4 + mate, y * 4 + across)
 
-    def near(a):
-        return y_near if a in (Q, G) else q_near
-
-    def near_slot(a):
-        return (up, down) if a in (Q, G) else (mate, across)
-
     def own_slot(a):
         return y if a in (Q, G) else xc
 
@@ -75,9 +69,9 @@
         pl.semaphore_signal(
             barrier, inc=1, device_id={"head": lax.rem(z + d, nz)}, device_id_type=MESH
         )
-    for frame in (*y_near, far * 4 + xc, *q_near):
+    for frame in (*y_near, far * 4 + xc, *q_near, y * 4 + corner):
         pl.semaphore_signal(barrier, inc=1, device_id={"frame": frame}, device_id_type=MESH)
-    pl.semaphore_wait(barrier, nz - 1 + 5)
+    pl.semaphore_wait(barrier, nz - 1 + 6)
 
     def a2a(a, d):
         to = lax.rem(z + d, nz)
@@ -114,53 +108,27 @@
         size = chunk if size is None else size
         return pl.ds(pl.multiple_of(start, size), size)
 
-    def near_copy(a, d, i):
-        here = allx.at[a, own_slot(a), span(d), :]
-        return remote(here, here, near_send.at[a, i], near_recv.at[a, i, d], near(a)[i])
-
-    def near_arrival(a, d, i):
-        there = allx.at[a, near_slot(a)[i], span(d), :]
-        back = 1 - i if a in (Q, G) else i
-        return remote(there, there, near_send.at[a, i], near_recv.at[a, back, d], near(a)[i])
-
-    def relay_copy(a, d, i):
-        half = chunk // 2
+    def partner(a, i):
         if a in (Q, G):
-            part = allx.at[a, near_slot(a)[1 - i], span(d, i * half, half), :]
-            return remote(part, part, relay_send.at[a, i], relay_recv.at[a, i], near(a)[i])
-        part = allx.at[a, across, span(d), :]
-        return remote(part, part, relay_send.at[a, 0], relay_recv.at[a, 0], q_near[0])
+            return (up, down, far)[i] * 4 + xc
+        return y * 4 + (mate, across, corner)[i]
 
     def pass_on(a, d, first=False):
         if first:
             own(a).wait()
         else:
             a2a(a, d).wait_recv()
-        for i in (0, 1):
-            near_copy(a, d, i).start()
-
-    def relay(a, d):
-        if a in (Q, G):
-            for i in (0, 1):
-                near_arrival(a, d, 1 - i).wait_recv()
-                relay_copy(a, d, i).start()
-        else:
-            near_arrival(a, d, 1).wait_recv()
-            relay_copy(a, d, 0).start()
-
-    def relay_total(a, i):
-        size = slab // 2 if a in (Q, G) else slab
-        part = allx.at[a, 0, 0:size, :]
-        return remote(part, part, relay_send.at[a, i], relay_recv.at[a, i], near(a)[i])
+        here = allx.at[a, own_slot(a), span(d), :]
+        for i in (2, 0, 1):
+            remote(here, here, near_send.at[a, i], near_recv.at[a, i], partner(a, i)).start()
+
+    def slab_total(a, i):
+        part = allx.at[a, own_slot(a)]
+        return remote(part, part, near_send.at[a, i], near_recv.at[a, i], partner(a, i))
 
     def arrived(a):
-        if a in (Q, G):
-            for i in (0, 1):
-                relay_total(a, i).wait_recv()
-        else:
-            for step in range(nz):
-                near_arrival(a, distance(step), 0).wait_recv()
-            relay_total(a, 0).wait_recv()
+        for i in (0, 1, 2):
+            slab_total(a, i).wait_recv()
 
     def bias_row(row, carry):
         h, qt = row // 8, lax.rem(row, 8)
@@ -171,18 +139,12 @@
             bias[row, :, kt * TILE:(kt + 1) * TILE] = jnp.full((8, TILE), value, F32)
         return carry
 
-    for a in (K, Q):
+    for a in (K, Q, V, G):
         pass_on(a, 0, True)
     lax.fori_loop(0, groups * 8, bias_row, 0)
     for step in range(1, nz):
         for a in (K, Q):
             pass_on(a, distance(step))
-        for a in (K, Q):
-            relay(a, distance(step - 1))
-    for a in (K, Q):
-        relay(a, distance(nz - 1))
-    for a in (V, G):
-        pass_on(a, 0, True)
     for a in (K, Q):
         arrived(a)
 
@@ -211,46 +173,38 @@
 
     rows[...] = jnp.zeros_like(rows)
 
-    def travel_step(step, carry):
-        for a in (V, G):
-            pass_on(a, distance(step))
-        for a in (V, G):
-            relay(a, distance(step - 1))
-
-        def one(unit, inner):
-            softmax_step(unit)
-            return inner
-
-        lax.fori_loop(2 * step - 2, 2 * step, one, 0)
-        return carry
-
-    lax.fori_loop(1, nz, travel_step, 0)
-    for a in (V, G):
-        relay(a, distance(nz - 1))
-
-    def rest(unit, carry):
-        softmax_step(unit)
-        return carry
-
-    lax.fori_loop(2 * nz - 2, groups * 4, rest, 0)
-
-    for s in range(4):
-        stats[y, :, s * slab:(s + 1) * slab] = rows[s].T[:16]
-
     def stat_copy(i, slot):
         frame = (up * 4 + xc, far * 4 + xc, down * 4 + xc)[i]
         part = stats.at[slot]
         return remote(part, part, st_send.at[i], st_recv.at[i], frame)
 
+    def share_stats():
+        for s in range(4):
+            stats[y, :, s * slab:(s + 1) * slab] = rows[s].T[:16]
+        for i in range(3):
+            stat_copy(i, y).start()
+
+    def one_unit(unit, carry):
+        softmax_step(unit)
+        return carry
+
+    units = groups * 4
+    done = 0
+    for step in range(1, nz):
+        for a in (V, G):
+            pass_on(a, distance(step))
+        if step % 2 == 0:
+            until = units if step >= nz - 2 else min(units, done + (6 if step == 2 else 9))
+            lax.fori_loop(done, until, one_unit, 0)
+            done = until
+        if step == nz - 2:
+            share_stats()
+
     def delta_copy(i, slot):
         frame = (up * 4 + xc, far * 4 + xc, down * 4 + xc)[i]
         part = deltas.at[slot]
         return remote(part, part, dl_send.at[i], dl_recv.at[i], frame)
 
-    for i in range(3):
-        stat_copy(i, y).start()
-    for a in (V, G):
-        arrived(a)
     for i in range(3):
         stat_copy(i, (down, far, up)[i]).wait_recv()
 
@@ -318,6 +272,9 @@
             parts[kind, across, h] = (mine + halves[kind, h].astype(F32)).astype(BF16)
             land_copy(kind, h, 1).start()
 
+    for a in (V, G):
+        arrived(a)
+
     def attend_head(h, carry):
         cols = column(h)
         value = allx[V, :, :, cols].reshape(4 * slab, HD)
@@ -415,11 +372,8 @@
     for a in (Q, K, V, G):
         for d in range(1, nz):
             a2a(a, d).wait_send()
-        for i in (0, 1):
-            part = allx.at[a, 0]
-            remote(part, part, near_send.at[a, i], relay_recv.at[a, 0], near(a)[i]).wait_send()
-        for i in (0, 1) if a in (Q, G) else (0,):
-            relay_total(a, i).wait_send()
+        for i in (0, 1, 2):
+            slab_total(a, i).wait_send()
     for i in range(3):
         stat_copy(i, y).wait_send()
         delta_copy(i, y).wait_send()
@@ -462,8 +416,8 @@
             pltpu.VMEM((4, 4, groups, slab, HD), BF16),
             pltpu.VMEM((4, groups, slab, HD), BF16),
             pltpu.VMEM((4, 2, groups, slab, HD), BF16),
-            dma((4, nz)), dma((4, nz)), dma((4,)), dma((4, 2)), dma((4, 2, nz)),
-            dma((4, 2)), dma((4, 2)), dma((3,)), dma((3,)), dma((3,)), dma((3,)),
+            dma((4, nz)), dma((4, nz)), dma((4,)), dma((4, 3)), dma((4, 3)),
+            dma((3,)), dma((3,)), dma((3,)), dma((3,)),
             dma((4, 2)), dma((4, groups, 2)), dma((4, 2)), dma((4, 2)),
         ],
         compiler_params=pltpu.CompilerParams(

time: 102 us -> 89 us (0.87)
  Pallas kernels: 96 us -> 83.1 us
    pallas_call x1, Pallas kernels: 96 us -> 83.1 us  [local(): pl.pallas_call(functools.partial(kernel, groups), out_shape=(out,) * 4, i...]
where the time goes in v3:
time: 89 us; the launch traced here: 88.5 us
  Pallas kernels  83.1 us (93%)
  local copies, waits for them, and re-layouts  4.68 us (5%)
    pallas_call x1, Pallas kernels, local(): pl.pallas_call(functools.partial(kernel, groups), out_shape=(out,) * 4, i...  83.1 us
    unnamed x10, local copies, waits for them, and re-layouts  4.68 us

profile of v3, /device:TPU:1, one launch (start us, length us, event | category | flops | bytes accessed | tf_op | source)
XLA Modules:
  0.0 88.5 jit_solution(5008625770209688668)
XLA Ops:
  0.6 83.1 %shard_map.84 = (bf16[256,640]{1,0:T(8,128)(2,1)}, bf16[256,640]{1,0:T(8,128)(2,1)}, bf16[256,640]{1,0:T(8,128)(2,1)}, bf16[256,640]{1,0:T(8,128)(2,1)}) custom-call(bf16[32,5120]{1,0:T(8,128)(2,1)} %q_hbm.1, bf16[32,5120]{1,0:T(8,128)(2,1)} %k_hbm.1, bf16[32,5120]{1,0:T(8,128)(2,1)} %v_hbm.1, bf16[32,5120]{1,0:T(8,128)(2,1)} %g_hbm.1, s32[5,32,32]{2,1,0:T(8,128)} %mask_ref.1), custom_call_target="tpu_custom_call" | custom-call | tf_op jit(solution)/shard_map/pallas_call | solution.py:400
  83.8 0.0 copy-start.2
  83.8 1.8 %copy.13 = bf16[256,640]{1,0:T(8,128)(2,1)} copy(bf16[256,640]{1,0:T(8,128)(2,1)} %get-tuple-element.8) | data formatting | bytes 655360
  85.5 0.0 copy-done.2
  85.6 0.0 copy-start.1
  85.6 0.7 copy.14
  86.3 0.4 copy-done.1
  86.6 0.0 copy-start
  86.6 0.7 copy.15
  87.4 0.4 copy-done
  87.7 0.7 copy.16
Async XLA Ops:
  83.8 1.8 %copy-start.2 = (bf16[256,640]{1,0:T(8,128)(2,1)S(1)}, bf16[256,640]{1,0:T(8,128)(2,1)}, u32[]{:S(2)}) copy-start(bf16[256,640]{1,0:T(8,128)(2,1)} %get-tuple-element.9) | copy-start | bytes 983044
  85.6 1.1 %copy-start.1 = (bf16[256,640]{1,0:T(8,128)(2,1)S(1)}, bf16[256,640]{1,0:T(8,128)(2,1)}, u32[]{:S(2)}) copy-start(bf16[256,640]{1,0:T(8,128)(2,1)} %get-tuple-element.10) | copy-start | bytes 983044
  86.6 1.1 %copy-start = (bf16[256,640]{1,0:T(8,128)(2,1)S(1)}, bf16[256,640]{1,0:T(8,128)(2,1)}, u32[]{:S(2)}) copy-start(bf16[256,640]{1,0:T(8,128)(2,1)} %get-tuple-element.11) | copy-start | bytes 983044

commit v4 on v3

--- a/solution.py
+++ b/solution.py
@@ -11,6 +11,7 @@
 HD = 128
 TILE = 128
 NEG = -1e30
+S2, S4, S6 = 2, 9, 6
 FLOOR = -1e20
 LOG2E = 1.4426950408889634
 MESH = pl.DeviceIdType.MESH
@@ -30,10 +31,11 @@
 
 def kernel(
     groups,
-    q_hbm, k_hbm, v_hbm, g_hbm, mask_ref,
+    q_hbm, k_hbm, v_hbm, g_hbm, mask_hbm,
     att_out, dq_out, dk_out, dv_out,
-    allx, probs, grads, bias, rows, stats, deltas, facts, shifts, scaled, parts, halves, landed,
-    a2a_send, a2a_recv, own_sem, near_send, near_recv,
+    mask_ref, allx, probs, bias, rows, stats, deltas, facts, shifts, scaled, parts, halves, landed, results,
+    result_sem,
+    mask_sem, a2a_send, a2a_recv, own_sem, near_send, near_recv,
     st_send, st_recv, dl_send, dl_recv, half_send, half_recv, land_send, land_recv,
 ):
     z = lax.axis_index("head")
@@ -64,6 +66,8 @@
             device_id={"frame": frame}, device_id_type=MESH,
         )
 
+    mask_copy = pltpu.make_async_copy(mask_hbm, mask_ref, mask_sem)
+    mask_copy.start()
     barrier = pltpu.get_barrier_semaphore()
     for d in range(1, nz):
         pl.semaphore_signal(
@@ -141,13 +145,11 @@
 
     for a in (K, Q, V, G):
         pass_on(a, 0, True)
+    mask_copy.wait()
     lax.fori_loop(0, groups * 8, bias_row, 0)
     for step in range(1, nz):
         for a in (K, Q):
             pass_on(a, distance(step))
-    for a in (K, Q):
-        arrived(a)
-
     lane = lax.broadcasted_iota(jnp.int32, (slab, HD), 1)
 
     def column(h):
@@ -193,12 +195,14 @@
     for step in range(1, nz):
         for a in (V, G):
             pass_on(a, distance(step))
-        if step % 2 == 0:
-            until = units if step >= nz - 2 else min(units, done + (6 if step == 2 else 9))
+        if step == 2:
+            for a in (K, Q):
+                arrived(a)
+        if step % 2 == 0 or step == nz - 1:
+            until = units if step == nz - 1 else min(units, done + {2: S2, 4: S4, 6: S6}.get(step, 0))
             lax.fori_loop(done, until, one_unit, 0)
             done = until
-        if step == nz - 2:
-            share_stats()
+    share_stats()
 
     def delta_copy(i, slot):
         frame = (up * 4 + xc, far * 4 + xc, down * 4 + xc)[i]
@@ -314,40 +318,39 @@
         block = jnp.concatenate([delta[:, s * slab:(s + 1) * slab], blank], axis=0)
         shifts[s] = block.T
 
-    def backward_head(h, carry):
+    def query_head(h, carry):
         cols = column(h)
 
-        def one(s, inner):
-            here = pl.ds(pl.multiple_of(s * slab, slab), slab)
+        value = allx[V, :, :, cols].reshape(4 * slab, HD)
+        key = allx[K, :, :, cols].reshape(4 * slab, HD)
+        for s in range(4):
             shift = pick(shifts[s], h)
-            value = allx[V, :, :, cols].reshape(4 * slab, HD)
-            key = allx[K, :, :, cols].reshape(4 * slab, HD)
-            moved = dot(scaled[h, here, :], value, NT)
+            moved = dot(scaled[h, s * slab:(s + 1) * slab, :], value, NT)
             score = (probs[h * 4 + s].astype(F32) * (moved - shift)).astype(BF16)
-            grads[here, :] = score
+            probs[h * 4 + s] = score
             parts[DQ, s, h] = (dot(score, key, NN) * scaling).astype(BF16)
-            return inner
-
-        lax.fori_loop(0, 4, one, 0)
         first_stage(DQ, h)
-        query = allx[Q, :, :, cols].reshape(4 * slab, HD)
-        turned = query.T
+        second_stage(DV, h)
+        return carry
+
+    lax.fori_loop(0, groups, query_head, 0)
+
+    def key_head(h, carry):
+        turned = allx[Q, :, :, column(h)].reshape(4 * slab, HD).T
+        score = probs[pl.ds(h * 4, 4)].reshape(4 * slab, 4 * slab)
         for t in range(4):
-            part = dot(turned, grads[:, t * slab:(t + 1) * slab], NN)
+            part = dot(turned, score[:, t * slab:(t + 1) * slab], NN)
             parts[DK, t, h] = (part.T * scaling).astype(BF16)
         first_stage(DK, h)
-        second_stage(DV, h)
+        second_stage(DQ, h)
 
         @pl.when(h > 0)
         def _():
-            second_stage(DQ, h - 1)
             second_stage(DK, h - 1)
 
         return carry
 
-    lax.fori_loop(0, groups, backward_head, 0)
-    second_stage(DQ, groups - 1)
-    second_stage(DK, groups - 1)
+    lax.fori_loop(0, groups, key_head, 0)
 
     def land_total(kind, i):
         frame = y_near[i] if kind in (ATT, DQ) else q_near[i]
@@ -359,7 +362,7 @@
         back = 1 - i if kind in (ATT, DQ) else i
         land_total(kind, back).wait_recv()
 
-    for kind, out in ((ATT, att_out), (DV, dv_out), (DK, dk_out), (DQ, dq_out)):
+    def finish(kind, out):
         for i in (0, 1):
             land_arrival(kind, i)
         slot = y if kind in (ATT, DQ) else xc
@@ -367,7 +370,16 @@
             value = parts[kind, slot, h].astype(F32)
             for i in (0, 1):
                 value += landed[kind, i, h].astype(F32)
-            out[:, h * HD:(h + 1) * HD] = value.astype(BF16)
+            results[kind, :, h * HD:(h + 1) * HD] = value.astype(BF16)
+        pltpu.make_async_copy(results.at[kind], out, result_sem.at[kind]).start()
+
+    finish(ATT, att_out)
+    second_stage(DK, groups - 1)
+    finish(DV, dv_out)
+    finish(DQ, dq_out)
+    finish(DK, dk_out)
+    for kind, out in ((ATT, att_out), (DV, dv_out), (DQ, dq_out), (DK, dk_out)):
+        pltpu.make_async_copy(results.at[kind], out, result_sem.at[kind]).wait()
 
     for a in (Q, K, V, G):
         for d in range(1, nz):
@@ -388,6 +400,19 @@
             land_total(kind, i).wait_send()
 
 
+def hand_over(*refs):
+    sources, targets, (held, in_sem, out_sem) = refs[:4], refs[4:8], refs[8:]
+    loads = [pltpu.make_async_copy(sources[i], held.at[i], in_sem.at[i]) for i in range(4)]
+    stores = [pltpu.make_async_copy(held.at[i], targets[i], out_sem.at[i]) for i in range(4)]
+    for load in loads:
+        load.start()
+    for load, store in zip(loads, stores):
+        load.wait()
+        store.start()
+    for store in stores:
+        store.wait()
+
+
 def local(queries, keys, values, out_grad, tile_mask):
     groups = tile_mask.shape[0]
     nz = lax.axis_size("head")
@@ -395,17 +420,16 @@
     units = groups * 4
     out = jax.ShapeDtypeStruct((slab, groups * HD), BF16)
     hbm = pl.BlockSpec(memory_space=pl.ANY)
-    vmem = pl.BlockSpec(memory_space=pltpu.VMEM)
     dma = pltpu.SemaphoreType.DMA
-    return pl.pallas_call(
+    results = pl.pallas_call(
         functools.partial(kernel, groups),
         out_shape=(out,) * 4,
-        in_specs=[hbm] * 4 + [pl.BlockSpec(memory_space=pltpu.SMEM)],
-        out_specs=(vmem,) * 4,
+        in_specs=[hbm] * 5,
+        out_specs=(hbm,) * 4,
         scratch_shapes=[
+            pltpu.SMEM(tile_mask.shape, jnp.int32),
             pltpu.VMEM((4, 4, slab, groups * HD), BF16),
             pltpu.VMEM((units, slab, 4 * slab), BF16),
-            pltpu.VMEM((4 * slab, 4 * slab), BF16),
             pltpu.VMEM((groups * 8, 8, 8 * TILE), F32),
             pltpu.VMEM((4, slab, HD), F32),
             pltpu.VMEM((4, 16, 4 * slab), F32),
@@ -416,14 +440,23 @@
             pltpu.VMEM((4, 4, groups, slab, HD), BF16),
             pltpu.VMEM((4, groups, slab, HD), BF16),
             pltpu.VMEM((4, 2, groups, slab, HD), BF16),
-            dma((4, nz)), dma((4, nz)), dma((4,)), dma((4, 3)), dma((4, 3)),
+            pltpu.VMEM((4, slab, groups * HD), BF16),
+            dma((4,)),
+            dma(()), dma((4, nz)), dma((4, nz)), dma((4,)), dma((4, 3)), dma((4, 3)),
             dma((3,)), dma((3,)), dma((3,)), dma((3,)),
             dma((4, 2)), dma((4, groups, 2)), dma((4, 2)), dma((4, 2)),
         ],
         compiler_params=pltpu.CompilerParams(
-            collective_id=0, has_side_effects=True, vmem_limit_bytes=56 << 20
+            collective_id=0, has_side_effects=True, vmem_limit_bytes=60 << 20
         ),
     )(queries, keys, values, out_grad, tile_mask)
+    return pl.pallas_call(
+        hand_over,
+        out_shape=(out,) * 4,
+        in_specs=[hbm] * 4,
+        out_specs=(hbm,) * 4,
+        scratch_shapes=[pltpu.VMEM((4, slab, groups * HD), BF16), dma((4,)), dma((4,))],
+    )(*results)
 
 
 def solution(mesh):

time: 89 us -> 82.2 us (0.924)
  local copies, waits for them, and re-layouts: 4.68 us -> 0 us
  Pallas kernels: 83.1 us -> 81.3 us
    unnamed x10 -> x0, local copies, waits for them, and re-layouts: 4.68 us -> none
    pallas_call x1, Pallas kernels: 83.1 us -> 79.3 us  [local(): pl.pallas_call(functools.partial(kernel, groups), out_shape=(out,) * 4, i...]
    pallas_call x0 -> x1, Pallas kernels: none -> 2.09 us  [local(): pl.pallas_call(hand_over, out_shape=(out,) * 4, in_specs=[hbm] * 4, out_s...]
where the time goes in v4:
time: 82.2 us; the launch traced here: 82 us
  Pallas kernels  81.3 us (99%)
    pallas_call x1, Pallas kernels, local(): pl.pallas_call(functools.partial(kernel, groups), out_shape=(out,) * 4, i...  79.3 us
    pallas_call x1, Pallas kernels, local(): pl.pallas_call(hand_over, out_shape=(out,) * 4, in_specs=[hbm] * 4, out_s...  2.09 us

profile of v4, /device:TPU:1, one launch (start us, length us, event | category | flops | bytes accessed | tf_op | source)
XLA Modules:
  0.0 82.0 jit_solution(13744190271248340535)
XLA Ops:
  0.6 79.3 %shard_map.84 = (bf16[256,640]{1,0:T(8,128)(2,1)}, bf16[256,640]{1,0:T(8,128)(2,1)}, bf16[256,640]{1,0:T(8,128)(2,1)}, bf16[256,640]{1,0:T(8,128)(2,1)}) custom-call(bf16[32,5120]{1,0:T(8,128)(2,1)} %q_hbm.1, bf16[32,5120]{1,0:T(8,128)(2,1)} %k_hbm.1, bf16[32,5120]{1,0:T(8,128)(2,1)} %v_hbm.1, bf16[32,5120]{1,0:T(8,128)(2,1)} %g_hbm.1, s32[5,32,32]{2,1,0:T(8,128)} %mask_hbm.1), custom_call_target="tpu_custom_call" | custom-call | tf_op jit(solution)/shard_map/pallas_call | solution.py:424
  79.9 2.1 %shard_map.85 = (bf16[256,640]{1,0:T(8,128)(2,1)}, bf16[256,640]{1,0:T(8,128)(2,1)}, bf16[256,640]{1,0:T(8,128)(2,1)}, bf16[256,640]{1,0:T(8,128)(2,1)}) custom-call(bf16[256,640]{1,0:T(8,128)(2,1)} %get-tuple-element.8.refs_0_, bf16[256,640]{1,0:T(8,128)(2,1)} %get-tuple-element.9.refs_1_, bf16[256,640]{1,0:T(8,128)(2,1)} %get-tuple-element.10.refs_2_, ...), custom_call_target="tpu_custom_call" | custom-call | tf_op jit(solution)/shard_map/pallas_call | solution.py:453

commit v5 on v4

--- a/solution.py
+++ b/solution.py
@@ -11,7 +11,7 @@
 HD = 128
 TILE = 128
 NEG = -1e30
-S2, S4, S6 = 2, 9, 6
+S2, S4, S6 = 2, 10, 6
 FLOOR = -1e20
 LOG2E = 1.4426950408889634
 MESH = pl.DeviceIdType.MESH
@@ -186,8 +186,9 @@
         for i in range(3):
             stat_copy(i, y).start()
 
-    def one_unit(unit, carry):
-        softmax_step(unit)
+    def one_unit(pair, carry):
+        softmax_step(2 * pair)
+        softmax_step(2 * pair + 1)
         return carry
 
     units = groups * 4
@@ -200,7 +201,7 @@
                 arrived(a)
         if step % 2 == 0 or step == nz - 1:
             until = units if step == nz - 1 else min(units, done + {2: S2, 4: S4, 6: S6}.get(step, 0))
-            lax.fori_loop(done, until, one_unit, 0)
+            lax.fori_loop(done // 2, until // 2, one_unit, 0)
             done = until
     share_stats()
 

time: 82.2 us -> 79.5 us (0.967)
  Pallas kernels: 81.3 us -> 78.6 us
    pallas_call x1, Pallas kernels: 79.3 us -> 76.6 us  [local(): pl.pallas_call(functools.partial(kernel, groups), out_shape=(out,) * 4, i...]
where the time goes in v5:
time: 79.5 us; the launch traced here: 79.3 us
  Pallas kernels  78.6 us (99%)
    pallas_call x1, Pallas kernels, local(): pl.pallas_call(functools.partial(kernel, groups), out_shape=(out,) * 4, i...  76.6 us
    pallas_call x1, Pallas kernels, local(): pl.pallas_call(hand_over, out_shape=(out,) * 4, in_specs=[hbm] * 4, out_s...  2.09 us

profile of v5, /device:TPU:1, one launch (start us, length us, event | category | flops | bytes accessed | tf_op | source)
XLA Modules:
  0.0 79.3 jit_solution(18156165289552760540)
XLA Ops:
  0.6 76.6 %shard_map.84 = (bf16[256,640]{1,0:T(8,128)(2,1)}, bf16[256,640]{1,0:T(8,128)(2,1)}, bf16[256,640]{1,0:T(8,128)(2,1)}, bf16[256,640]{1,0:T(8,128)(2,1)}) custom-call(bf16[32,5120]{1,0:T(8,128)(2,1)} %q_hbm.1, bf16[32,5120]{1,0:T(8,128)(2,1)} %k_hbm.1, bf16[32,5120]{1,0:T(8,128)(2,1)} %v_hbm.1, bf16[32,5120]{1,0:T(8,128)(2,1)} %g_hbm.1, s32[5,32,32]{2,1,0:T(8,128)} %mask_hbm.1), custom_call_target="tpu_custom_call" | custom-call | tf_op jit(solution)/shard_map/pallas_call | solution.py:425
  77.2 2.1 %shard_map.85 = (bf16[256,640]{1,0:T(8,128)(2,1)}, bf16[256,640]{1,0:T(8,128)(2,1)}, bf16[256,640]{1,0:T(8,128)(2,1)}, bf16[256,640]{1,0:T(8,128)(2,1)}) custom-call(bf16[256,640]{1,0:T(8,128)(2,1)} %get-tuple-element.8.refs_0_, bf16[256,640]{1,0:T(8,128)(2,1)} %get-tuple-element.9.refs_1_, bf16[256,640]{1,0:T(8,128)(2,1)} %get-tuple-element.10.refs_2_, ...), custom_call_target="tpu_custom_call" | custom-call | tf_op jit(solution)/shard_map/pallas_call | solution.py:454

commit v6 on v5

--- a/solution.py
+++ b/solution.py
@@ -11,7 +11,7 @@
 HD = 128
 TILE = 128
 NEG = -1e30
-S2, S4, S6 = 2, 10, 6
+S2, S4, S6 = 0, 10, 6
 FLOOR = -1e20
 LOG2E = 1.4426950408889634
 MESH = pl.DeviceIdType.MESH

time: 79.5 us -> 80.7 us (1.015)
  Pallas kernels: 78.6 us -> 79.9 us
    pallas_call x1, Pallas kernels: 76.6 us -> 77.8 us  [local(): pl.pallas_call(functools.partial(kernel, groups), out_shape=(out,) * 4, i...]
where the time goes in v6:
time: 80.7 us; the launch traced here: 80.5 us
  Pallas kernels  79.9 us (99%)
    pallas_call x1, Pallas kernels, local(): pl.pallas_call(functools.partial(kernel, groups), out_shape=(out,) * 4, i...  77.8 us
    pallas_call x1, Pallas kernels, local(): pl.pallas_call(hand_over, out_shape=(out,) * 4, in_specs=[hbm] * 4, out_s...  2.09 us

profile of v6, /device:TPU:1, one launch (start us, length us, event | category | flops | bytes accessed | tf_op | source)
XLA Modules:
  0.0 80.5 jit_solution(7346698607664010680)
XLA Ops:
  0.6 77.8 %shard_map.84 = (bf16[256,640]{1,0:T(8,128)(2,1)}, bf16[256,640]{1,0:T(8,128)(2,1)}, bf16[256,640]{1,0:T(8,128)(2,1)}, bf16[256,640]{1,0:T(8,128)(2,1)}) custom-call(bf16[32,5120]{1,0:T(8,128)(2,1)} %q_hbm.1, bf16[32,5120]{1,0:T(8,128)(2,1)} %k_hbm.1, bf16[32,5120]{1,0:T(8,128)(2,1)} %v_hbm.1, bf16[32,5120]{1,0:T(8,128)(2,1)} %g_hbm.1, s32[5,32,32]{2,1,0:T(8,128)} %mask_hbm.1), custom_call_target="tpu_custom_call" | custom-call | tf_op jit(solution)/shard_map/pallas_call | solution.py:425
  78.4 2.1 %shard_map.85 = (bf16[256,640]{1,0:T(8,128)(2,1)}, bf16[256,640]{1,0:T(8,128)(2,1)}, bf16[256,640]{1,0:T(8,128)(2,1)}, bf16[256,640]{1,0:T(8,128)(2,1)}) custom-call(bf16[256,640]{1,0:T(8,128)(2,1)} %get-tuple-element.8.refs_0_, bf16[256,640]{1,0:T(8,128)(2,1)} %get-tuple-element.9.refs_1_, bf16[256,640]{1,0:T(8,128)(2,1)} %get-tuple-element.10.refs_2_, ...), custom_call_target="tpu_custom_call" | custom-call | tf_op jit(solution)/shard_map/pallas_call | solution.py:454

commit v7 on v5

--- a/solution.py
+++ b/solution.py
@@ -403,8 +403,14 @@
 
 def hand_over(*refs):
     sources, targets, (held, in_sem, out_sem) = refs[:4], refs[4:8], refs[8:]
-    loads = [pltpu.make_async_copy(sources[i], held.at[i], in_sem.at[i]) for i in range(4)]
-    stores = [pltpu.make_async_copy(held.at[i], targets[i], out_sem.at[i]) for i in range(4)]
+    half = held.shape[1] // 2
+    cuts = [(i, j, pl.ds(j * half, half)) for i in range(4) for j in (0, 1)]
+    loads = [
+        pltpu.make_async_copy(sources[i].at[c], held.at[i, c], in_sem.at[i, j]) for i, j, c in cuts
+    ]
+    stores = [
+        pltpu.make_async_copy(held.at[i, c], targets[i].at[c], out_sem.at[i, j]) for i, j, c in cuts
+    ]
     for load in loads:
         load.start()
     for load, store in zip(loads, stores):
@@ -456,7 +462,7 @@
         out_shape=(out,) * 4,
         in_specs=[hbm] * 4,
         out_specs=(hbm,) * 4,
-        scratch_shapes=[pltpu.VMEM((4, slab, groups * HD), BF16), dma((4,)), dma((4,))],
+        scratch_shapes=[pltpu.VMEM((4, slab, groups * HD), BF16), dma((4, 2)), dma((4, 2))],
     )(*results)
 
 

time: 79.5 us -> 79.6 us (level)
  no operation moved by 1% of the time
where the time goes in v7:
time: 79.6 us; the launch traced here: 79.4 us
  Pallas kernels  78.8 us (99%)
    pallas_call x1, Pallas kernels, local(): pl.pallas_call(functools.partial(kernel, groups), out_shape=(out,) * 4, i...  76.6 us
    pallas_call x1, Pallas kernels, local(): pl.pallas_call(hand_over, out_shape=(out,) * 4, in_specs=[hbm] * 4, out_s...  2.21 us

profile of v7, /device:TPU:1, one launch (start us, length us, event | category | flops | bytes accessed | tf_op | source)
XLA Modules:
  0.0 79.4 jit_solution(1033853391119437467)
XLA Ops:
  0.6 76.6 %shard_map.84 = (bf16[256,640]{1,0:T(8,128)(2,1)}, bf16[256,640]{1,0:T(8,128)(2,1)}, bf16[256,640]{1,0:T(8,128)(2,1)}, bf16[256,640]{1,0:T(8,128)(2,1)}) custom-call(bf16[32,5120]{1,0:T(8,128)(2,1)} %q_hbm.1, bf16[32,5120]{1,0:T(8,128)(2,1)} %k_hbm.1, bf16[32,5120]{1,0:T(8,128)(2,1)} %v_hbm.1, bf16[32,5120]{1,0:T(8,128)(2,1)} %g_hbm.1, s32[5,32,32]{2,1,0:T(8,128)} %mask_hbm.1), custom_call_target="tpu_custom_call" | custom-call | tf_op jit(solution)/shard_map/pallas_call | solution.py:431
  77.2 2.2 %shard_map.85 = (bf16[256,640]{1,0:T(8,128)(2,1)}, bf16[256,640]{1,0:T(8,128)(2,1)}, bf16[256,640]{1,0:T(8,128)(2,1)}, bf16[256,640]{1,0:T(8,128)(2,1)}) custom-call(bf16[256,640]{1,0:T(8,128)(2,1)} %get-tuple-element.8.refs_0_, bf16[256,640]{1,0:T(8,128)(2,1)} %get-tuple-element.9.refs_1_, bf16[256,640]{1,0:T(8,128)(2,1)} %get-tuple-element.10.refs_2_, ...), custom_call_target="tpu_custom_call" | custom-call | tf_op jit(solution)/shard_map/pallas_call | solution.py:460
